TPU v7x, 256 devices: a whole 4x4x8 slice. The times are simulated.
256 devices in a mesh: dp: 16 (over x_lo, z), tensor: 16 (over y, x_hi, core).
Axes of the slice: x: 4 (x_hi: 2, x_lo: 2; x = x_hi * 2 + x_lo), y: 4, z: 8, core: 2. Of those that a mesh axis runs over, the one named last changes fastest.
Arguments:
- query_rows: bfloat16 [32768, 8192], P('dp', 'tensor'), may hold values from -16 to 16
- key_rows: bfloat16 [32768, 1024], P('dp'), may hold values from -10 to 10
- value_rows: bfloat16 [32768, 1024], P('dp'), may hold values from -600 to 600
- segment_ids: int32 [32768], P('dp'), may hold values from 0 to 127, never falling along the last dimension, each value on 1 to 512 neighbouring positions
- norm_gain: float32 [8192], replicated, may hold values from 0.1 to 1.9
- draft_weight: bfloat16 [8192, 512], P('tensor', 'dp'), may hold values from -0.0625 to 0.0625
- targets: bfloat16 [32768, 512], P(('dp', 'tensor')), may hold values from -6 to 6
Outputs:
- grad_weight: float32 [8192, 512], P('tensor', 'dp')
Inputs may be any that keep to these rules, and one draw needn't show every extreme that they name: `segment_ids`: document ids never fall along the tokens; a document has at most 512 tokens, and one has exactly 512.
All inputs are finite; a program needn't handle non-finite values.
Results may differ from a plain program's by a relative error of at most 0.0015.
Values may be sent and summed in bfloat16 or wider, within the bound.
No kernel may reach another device: no remote copies, remote signals or barrier semaphores. Data moves between devices by JAX's collectives and lax.ppermute only.
A program may use at most 128 MiB of HBM per device.

v0:
```python
import jax
import jax.numpy as jnp
from jax import lax
from jax.sharding import PartitionSpec as P

HEADS = 64
KV_HEADS = 8
HEAD_DIM = 128


def attend_local(query_rows, key_rows, value_rows, segment_ids):
    length = query_rows.shape[0]
    local_heads = query_rows.shape[1] // HEAD_DIM
    group = HEADS // KV_HEADS
    head_count = max(1, local_heads // group)
    repeats = local_heads // head_count
    first = lax.axis_index("tensor") * local_heads // group
    keys_local = lax.dynamic_slice_in_dim(
        key_rows, first * HEAD_DIM, head_count * HEAD_DIM, 1
    ).reshape(length, head_count, HEAD_DIM)
    values_local = lax.dynamic_slice_in_dim(
        value_rows, first * HEAD_DIM, head_count * HEAD_DIM, 1
    ).reshape(length, head_count, HEAD_DIM)
    grouped = query_rows.reshape(length, head_count, repeats, HEAD_DIM)
    width = min(length, 512)
    scale = HEAD_DIM ** (-0.5)
    places = jnp.arange(length, dtype=jnp.int32)

    def one_block(number):
        offset = number * width
        query_block = lax.dynamic_slice_in_dim(grouped, offset, width, 0)
        block_segments = lax.dynamic_slice_in_dim(segment_ids, offset, width, 0)
        block_places = offset + jnp.arange(width, dtype=jnp.int32)
        allowed = (block_segments[:, None] == segment_ids[None, :]) & (
            block_places[:, None] >= places[None, :]
        )
        scores = (
            jnp.einsum(
                "qgrd,kgd->grqk", query_block, keys_local, preferred_element_type=jnp.float32
            )
            * scale
        )
        scores = jnp.where(allowed[None, None], scores, -1e30)
        shifted = jnp.exp(scores - jnp.max(scores, axis=-1, keepdims=True))
        probs = (shifted / jnp.sum(shifted, axis=-1, keepdims=True)).astype(jnp.bfloat16)
        mixed = jnp.einsum(
            "grqk,kgd->qgrd", probs, values_local, preferred_element_type=jnp.float32
        )
        return mixed.astype(jnp.bfloat16).reshape(width, local_heads * HEAD_DIM)

    outputs = lax.map(one_block, jnp.arange(length // width, dtype=jnp.int32))
    return outputs.reshape(length, local_heads * HEAD_DIM)


def loss_derivative(predicted, targets, total_tokens):
    residual = predicted - targets.astype(jnp.float32)
    return (jnp.clip(residual, -1.0, 1.0) / jnp.sqrt(jnp.float32(total_tokens))).astype(
        jnp.bfloat16
    )


def on_device(query_rows, key_rows, value_rows, segment_ids, norm_gain, draft_weight, targets):
    attended = attend_local(query_rows, key_rows, value_rows, segment_ids)
    length = query_rows.shape[0]
    total_tokens = length * lax.axis_size("dp")
    weight_slab = lax.all_gather(draft_weight, "dp", axis=1, tiled=True)
    regrouped = lax.all_to_all(attended, "tensor", split_axis=0, concat_axis=1, tiled=True)
    features = regrouped.astype(jnp.float32)
    mean_square = jnp.mean(features * features, axis=-1, keepdims=True)
    normed = (features * lax.rsqrt(mean_square + 1e-06) * norm_gain[None, :]).astype(jnp.bfloat16)
    picked = normed
    predicted = jnp.dot(
        picked,
        lax.all_gather(weight_slab, "tensor", axis=0, tiled=True),
        preferred_element_type=jnp.float32,
    )
    grad_pred = loss_derivative(predicted, targets, total_tokens)
    picked = normed
    grad_slab = lax.psum_scatter(
        lax.dot_general(
            picked, grad_pred, (((0,), (0,)), ((), ())), preferred_element_type=jnp.float32
        ),
        "tensor",
        scatter_dimension=0,
        tiled=True,
    )
    return lax.psum_scatter(grad_slab, "dp", scatter_dimension=1, tiled=True)


def solution(mesh):
    placed = (
        P("dp", "tensor"),
        P("dp", None),
        P("dp", None),
        P("dp"),
        P(),
        P("tensor", "dp"),
        P(("dp", "tensor"), None),
    )
    return jax.shard_map(
        on_device, mesh=mesh, in_specs=placed, out_specs=P("tensor", "dp"), check_vma=False
    )
```

profile of v0, /device:TPU:32, one launch (start us, length us, event | category | flops | bytes accessed | tf_op | source)
XLA Modules:
  0.0 411.7 jit_solution(10289684197386694751)
XLA Ops:
  6.5 38.9 %all_gather.6 = bf16[512,512]{0,1:T(8,128)(2,1)} all-gather(bf16[512,32]{0,1:T(8,128)(2,1)} %param.14), channel_id=1, replica_groups=mesh['dp'=16,'tensor'=16] {'dp'}, dimensions={1}, use_global_device_ids=true | all-gather | bytes 557056 | tf_op jit(solution)/shard_map/all_gather | solution.py:66
  45.6 1.1 constant_dynamic-slice_fusion
  46.7 0.2 copy.17
  46.9 1.1 dynamic-slice_bitcast_fusion
  48.0 2.5 copy.16
  50.5 73.3 %while.11 = (s32[]{:T(128)}, bf16[4,512,512]{2,1,0:T(8,128)(2,1)}, s32[4]{0:T(128)S(1)}, s32[2048]{0:T(1024)S(1)}, bf16[2048,1,4,128]{0,3,2,1:T(8,128)(2,1)}, /*...) while((s32[]{:T(128)}, bf16[4,512,512]{2,1,0:T(8,128)(2,1)}, ...), condition=%wide.region_3.4_spmd.clone, body=%wide.region_0.3_spmd.clone.sunk | while | flops 2201219584 | bytes 58780336 | solution.py:51
  50.5 0.6 dynamic_slice.33
  51.9 0.1 dynamic_slice.34
  51.9 1.2 fusion.37
  53.1 4.9 %fusion.38 = (f32[4,512]{1,0:T(4,128)S(1)}, f32[512,4,2048]{2,0,1:T(8,128)S(1)}) fusion(pred[512,2048]{1,0:T(8,128)(4,1)S(1)} %fusion.37, bf16[2048,1,128]{2,0,1:T(8,128)(2,1)S(1)} %get-tuple-element.168, bf16[2048,1,4,128]{0,3,2,1:T(8,128)(2,1)} %get-tuple-element.167, s32[]{:T(128)S(6)} %select_n.40), kind=kOutput, calls=%fused_computation.5.clone.1 | convolution fusion | flops 1086322688 | bytes 18882564 | tf_op jit(solution)/shard_map/while/body/eval_jaxpr/qgrd,kgd->grqk/dot_general | solution.py:38
  58.0 4.5 %fusion.39 = f32[4,512]{1,0:T(4,128)S(1)} fusion(f32[512,4,2048]{2,0,1:T(8,128)S(1)} %get-tuple-element.139, f32[4,512]{1,0:T(4,128)S(1)} %get-tuple-element.140, pred[512,2048]{1,0:T(8,128)(4,1)S(1)} %fusion.37), kind=kLoop, calls=%fused_computation.4.clone.1 | loop fusion | flops 16775168 | bytes 17842176 | tf_op jit(solution)/shard_map/while/body/eval_jaxpr/reduce_sum | solution.py:45
  62.5 5.3 %fusion.40 = bf16[4,512,128]{1,2,0:T(8,128)(2,1)S(1)} fusion(f32[4,512]{1,0:T(4,128)S(1)} %fusion.39, f32[4,512]{1,0:T(4,128)S(1)} %get-tuple-element.140, f32[512,4,2048]{2,0,1:T(8,128)S(1)} %get-tuple-element.139, pred[512,2048]{1,0:T(8,128)(4,1)S(1)} %fusion.37, bf16[2048,1,128]{0,2,1:T(8,128)(2,1)S(1)} %get-tuple-element.169), kind=kOutput, calls=%fused_computation.10.clone.1 | convolution fusion | flops 1094975488 | bytes 18890752 | tf_op jit(solution)/shard_map/while/body/eval_jaxpr/grqk,kgd->qgrd/dot_general | solution.py:46
  67.8 0.2 copy.28
  68.0 0.9 constant_dynamic-update-slice_fusion.2
  68.9 0.6 dynamic_slice.33
  70.2 0.1 dynamic_slice.34
  70.3 1.2 fusion.37
  71.5 4.9 %fusion.38 = (f32[4,512]{1,0:T(4,128)S(1)}, f32[512,4,2048]{2,0,1:T(8,128)S(1)}) fusion(pred[512,2048]{1,0:T(8,128)(4,1)S(1)} %fusion.37, bf16[2048,1,128]{2,0,1:T(8,128)(2,1)S(1)} %get-tuple-element.168, bf16[2048,1,4,128]{0,3,2,1:T(8,128)(2,1)} %get-tuple-element.167, s32[]{:T(128)S(6)} %select_n.40), kind=kOutput, calls=%fused_computation.5.clone.1 | convolution fusion | flops 1086322688 | bytes 18882564 | tf_op jit(solution)/shard_map/while/body/eval_jaxpr/qgrd,kgd->grqk/dot_general | solution.py:38
  76.4 4.5 %fusion.39 = f32[4,512]{1,0:T(4,128)S(1)} fusion(f32[512,4,2048]{2,0,1:T(8,128)S(1)} %get-tuple-element.139, f32[4,512]{1,0:T(4,128)S(1)} %get-tuple-element.140, pred[512,2048]{1,0:T(8,128)(4,1)S(1)} %fusion.37), kind=kLoop, calls=%fused_computation.4.clone.1 | loop fusion | flops 16775168 | bytes 17842176 | tf_op jit(solution)/shard_map/while/body/eval_jaxpr/reduce_sum | solution.py:45
  80.8 5.3 %fusion.40 = bf16[4,512,128]{1,2,0:T(8,128)(2,1)S(1)} fusion(f32[4,512]{1,0:T(4,128)S(1)} %fusion.39, f32[4,512]{1,0:T(4,128)S(1)} %get-tuple-element.140, f32[512,4,2048]{2,0,1:T(8,128)S(1)} %get-tuple-element.139, pred[512,2048]{1,0:T(8,128)(4,1)S(1)} %fusion.37, bf16[2048,1,128]{0,2,1:T(8,128)(2,1)S(1)} %get-tuple-element.169), kind=kOutput, calls=%fused_computation.10.clone.1 | convolution fusion | flops 1094975488 | bytes 18890752 | tf_op jit(solution)/shard_map/while/body/eval_jaxpr/grqk,kgd->qgrd/dot_general | solution.py:46
  86.1 0.2 copy.28
  86.4 0.8 constant_dynamic-update-slice_fusion.2
  87.2 0.6 dynamic_slice.33
  88.5 0.1 dynamic_slice.34
  88.6 1.2 fusion.37
  89.8 4.9 %fusion.38 = (f32[4,512]{1,0:T(4,128)S(1)}, f32[512,4,2048]{2,0,1:T(8,128)S(1)}) fusion(pred[512,2048]{1,0:T(8,128)(4,1)S(1)} %fusion.37, bf16[2048,1,128]{2,0,1:T(8,128)(2,1)S(1)} %get-tuple-element.168, bf16[2048,1,4,128]{0,3,2,1:T(8,128)(2,1)} %get-tuple-element.167, s32[]{:T(128)S(6)} %select_n.40), kind=kOutput, calls=%fused_computation.5.clone.1 | convolution fusion | flops 1086322688 | bytes 18882564 | tf_op jit(solution)/shard_map/while/body/eval_jaxpr/qgrd,kgd->grqk/dot_general | solution.py:38
  94.7 4.5 %fusion.39 = f32[4,512]{1,0:T(4,128)S(1)} fusion(f32[512,4,2048]{2,0,1:T(8,128)S(1)} %get-tuple-element.139, f32[4,512]{1,0:T(4,128)S(1)} %get-tuple-element.140, pred[512,2048]{1,0:T(8,128)(4,1)S(1)} %fusion.37), kind=kLoop, calls=%fused_computation.4.clone.1 | loop fusion | flops 16775168 | bytes 17842176 | tf_op jit(solution)/shard_map/while/body/eval_jaxpr/reduce_sum | solution.py:45
  99.2 5.3 %fusion.40 = bf16[4,512,128]{1,2,0:T(8,128)(2,1)S(1)} fusion(f32[4,512]{1,0:T(4,128)S(1)} %fusion.39, f32[4,512]{1,0:T(4,128)S(1)} %get-tuple-element.140, f32[512,4,2048]{2,0,1:T(8,128)S(1)} %get-tuple-element.139, pred[512,2048]{1,0:T(8,128)(4,1)S(1)} %fusion.37, bf16[2048,1,128]{0,2,1:T(8,128)(2,1)S(1)} %get-tuple-element.169), kind=kOutput, calls=%fused_computation.10.clone.1 | convolution fusion | flops 1094975488 | bytes 18890752 | tf_op jit(solution)/shard_map/while/body/eval_jaxpr/grqk,kgd->qgrd/dot_general | solution.py:46
  104.5 0.2 copy.28
  104.7 0.8 constant_dynamic-update-slice_fusion.2
  105.5 0.6 dynamic_slice.33
  106.9 0.1 dynamic_slice.34
  106.9 1.2 fusion.37
  108.1 4.9 %fusion.38 = (f32[4,512]{1,0:T(4,128)S(1)}, f32[512,4,2048]{2,0,1:T(8,128)S(1)}) fusion(pred[512,2048]{1,0:T(8,128)(4,1)S(1)} %fusion.37, bf16[2048,1,128]{2,0,1:T(8,128)(2,1)S(1)} %get-tuple-element.168, bf16[2048,1,4,128]{0,3,2,1:T(8,128)(2,1)} %get-tuple-element.167, s32[]{:T(128)S(6)} %select_n.40), kind=kOutput, calls=%fused_computation.5.clone.1 | convolution fusion | flops 1086322688 | bytes 18882564 | tf_op jit(solution)/shard_map/while/body/eval_jaxpr/qgrd,kgd->grqk/dot_general | solution.py:38
  113.0 4.5 %fusion.39 = f32[4,512]{1,0:T(4,128)S(1)} fusion(f32[512,4,2048]{2,0,1:T(8,128)S(1)} %get-tuple-element.139, f32[4,512]{1,0:T(4,128)S(1)} %get-tuple-element.140, pred[512,2048]{1,0:T(8,128)(4,1)S(1)} %fusion.37), kind=kLoop, calls=%fused_computation.4.clone.1 | loop fusion | flops 16775168 | bytes 17842176 | tf_op jit(solution)/shard_map/while/body/eval_jaxpr/reduce_sum | solution.py:45
  117.5 5.3 %fusion.40 = bf16[4,512,128]{1,2,0:T(8,128)(2,1)S(1)} fusion(f32[4,512]{1,0:T(4,128)S(1)} %fusion.39, f32[4,512]{1,0:T(4,128)S(1)} %get-tuple-element.140, f32[512,4,2048]{2,0,1:T(8,128)S(1)} %get-tuple-element.139, pred[512,2048]{1,0:T(8,128)(4,1)S(1)} %fusion.37, bf16[2048,1,128]{0,2,1:T(8,128)(2,1)S(1)} %get-tuple-element.169), kind=kOutput, calls=%fused_computation.10.clone.1 | convolution fusion | flops 1094975488 | bytes 18890752 | tf_op jit(solution)/shard_map/while/body/eval_jaxpr/grqk,kgd->qgrd/dot_general | solution.py:46
  122.8 0.2 copy.28
  123.0 0.9 constant_dynamic-update-slice_fusion.2
  123.9 35.9 %all_to_all.13 = bf16[16,128,512]{2,1,0:T(8,128)(2,1)S(1)} all-to-all(bf16[16,128,512]{2,1,0:T(8,128)(2,1)} %bitcast.86), channel_id=1, replica_groups=mesh['dp'=16,'tensor'=16] {'tensor'}, dimensions={0} | all-to-all | bytes 4194304 | tf_op jit(solution)/shard_map/all_to_all | solution.py:67
  159.8 2.5 convert_bitcast_fusion
  162.3 5.3 %copy.20 = f32[128,16,512]{0,2,1:T(8,128)} copy(f32[128,16,512]{2,0,1:T(8,128)} %convert_bitcast_fusion) | data formatting | bytes 8388608 | tf_op jit(solution)/shard_map/convert_element_type | solution.py:68
  167.7 0.5 fusion.18
  168.2 2.9 fusion.20
  171.1 6.3 %fusion.23 = bf16[128,512]{1,0:T(8,128)(2,1)S(1)} fusion(bf16[128,8192]{0,1:T(8,128)(2,1)S(1)} %fusion.20, bf16[8192,512]{0,1:T(8,128)(2,1)} %all-gather.2.cloned.1.call-done, bf16[128,512]{1,0:T(8,128)(2,1)S(1)} %copy-done.2), kind=kOutput, calls=%fused_computation.30 | convolution fusion | flops 1074069504 | bytes 10747904 | tf_op jit(solution)/shard_map/dot_general | solution.py:72
  177.4 8.0 %fusion.24 = f32[8192,512]{1,0:T(8,128)} fusion(bf16[128,8192]{0,1:T(8,128)(2,1)S(1)} %fusion.20, bf16[128,512]{1,0:T(8,128)(2,1)S(1)} %fusion.23), kind=kOutput, calls=%fused_computation.34 | convolution fusion | flops 1073741824 | bytes 19005440 | tf_op jit(solution)/shard_map/dot_general | solution.py:80
  185.5 149.0 %reduce-scatter.5.cloned.1.call-done = f32[512,512]{1,0:T(8,128)} async-done(((f32[8192,512]{1,0:T(8,128)}), f32[512,512]{1,0:T(8,128)}) %reduce-scatter.5.cloned.1.call-update) | async-done | bytes 1048592 | tf_op jit(solution)/shard_map/reduce_scatter | solution.py:79
  334.5 2.5 copy.22
  337.1 68.1 %reduce-scatter.7.cloned.1.call-done = f32[32,512]{1,0:T(8,128)} async-done(((f32[512,512]{1,0:T(8,128)}), f32[32,512]{1,0:T(8,128)}) %reduce-scatter.7.cloned.1.call-update) | async-done | bytes 65552
  (22 shorter events, 0.2 us)
Async XLA Ops:
  6.5 41.5 %copy-start = (bf16[2048,512]{1,0:T(8,128)(2,1)S(1)}, bf16[2048,512]{1,0:T(8,128)(2,1)}, u32[]{:S(2)}) copy-start(bf16[2048,512]{1,0:T(8,128)(2,1)} %param.9) | copy-start | bytes 6291460
  6.5 44.0 %copy-start.1 = (s32[2048]{0:T(1024)S(1)}, s32[2048]{0:T(1024)}, u32[]{:S(2)}) copy-start(s32[2048]{0:T(1024)} %param.12) | copy-start | bytes 24580
  6.5 164.5 %all-gather.2.cloned.1.call-start = ((), (), s32[]{:S(2)}) async-start(), calls=%async_computation.3 | async-start | bytes 8912896 | tf_op jit(solution)/shard_map/all_gather | solution.py:74
  45.5 289.0 %reduce-scatter.5.cloned.1.call-start = ((), (), s32[]{:S(2)}) async-start(), calls=%async_computation.4 | async-start | bytes 17825792 | tf_op jit(solution)/shard_map/reduce_scatter | solution.py:79
  162.3 5.9 %copy-start.3 = (f32[8192]{0:T(1024)S(1)}, f32[8192]{0:T(1024)}, u32[]{:S(2)}) copy-start(f32[8192]{0:T(1024)} %param.13) | copy-start | bytes 98308
  167.7 3.4 copy-start.2
  185.4 219.7 %reduce-scatter.7.cloned.1.call-start = ((), (), s32[]{:S(2)}) async-start(), calls=%async_computation.5 | async-start | bytes 1114112
Sparse Core Ops, SparseCore 0:
  45.6 79.9 all-gather.1
  185.6 148.9 reduce-scatter.4
  337.2 67.8 reduce-scatter.6
where the time goes:
time: 415 us; the launch traced here: 412 us
  waiting for transfers between devices  217 us (52%)
  blocking collectives  74.9 us (18%)
  matrix products  55 us (13%)
  other arithmetic  28.6 us (7%)
  local copies, waits for them, and re-layouts  20 us (5%)
  between operations  13.2 us (3%)
    reduce_scatter x1, waiting for transfers between devices, on_device(): lax.psum_scatter(lax.dot_general(picked, grad_pred, (((0,), (0,)), ((), (...  149 us
    unnamed x4, waiting for transfers between devices  68.1 us
    all_gather x1, blocking collectives, on_device(): weight_slab = lax.all_gather(draft_weight, 'dp', axis=1, tiled=True)  38.9 us
    all_to_all x1, blocking collectives, on_device(): lax.all_to_all(attended, 'tensor', split_axis=0, concat_axis=1, tiled=True)  35.9 us
    dot_general x4, matrix products, one_block(): jnp.einsum('grqk,kgd->qgrd', probs, values_local, preferred_element_type=...  21.1 us
    dot_general x4, matrix products, one_block(): jnp.einsum('qgrd,kgd->grqk', query_block, keys_local, preferred_element_t...  19.5 us
    reduce_sum x4, other arithmetic, one_block(): jnp.sum(shifted, axis=-1, keepdims=True)  17.9 us
  transfers between devices with their start and end apart: 3, of which 2 were waited for; matrix products, arithmetic and copies ran while one was open for 21% of the time, Pallas kernels for 0%

commit v1 on v0

v1 whole, which is shorter than its diff:
```python
import math

import jax
import jax.numpy as jnp
from jax import lax
from jax.experimental import pallas as pl
from jax.experimental.pallas import tpu as pltpu
from jax.sharding import PartitionSpec as P

HEADS = 64
KV_HEADS = 8
HEAD_DIM = 128
DOC_MAX = 512
BLOCK = 128
EXTRA = 16
BF16 = jnp.bfloat16
F32 = jnp.float32
F16 = jnp.float16
ROOT_SCALE = 2.0**20


def scalar_rows(x):
    rows = lax.broadcasted_iota(jnp.int32, (EXTRA, BLOCK), 0)
    high = x.astype(BF16).astype(F32)
    rest = x - high
    middle = rest.astype(BF16).astype(F32)
    low = rest - middle
    return jnp.where(
        rows == 0, high, jnp.where(rows == 1, middle, jnp.where(rows == 2, low, 0.0))
    ).astype(BF16)


def scalar_of(rows):
    return jnp.sum(rows.astype(F32), axis=0, keepdims=True)


def attention(
    places, segment_ids, first, count, query_rows, key_rows, value_rows, segments,
    weight=None, gains=None,
):
    length, width = query_rows.shape
    heads = width // HEAD_DIM
    blocks = length // BLOCK
    most = min(blocks, DOC_MAX // BLOCK + 1)
    step = math.log2(math.e) * HEAD_DIM ** (-0.5)

    def body(place, ids, *refs):
        query, key, value, segment = refs[:4]
        out, square = refs[-2:] if weight is None else refs[-3:-1]
        block = (first + pl.program_id(0)) * 2 + place[0]
        needed = 1
        for back in range(1, most):
            end = jnp.maximum((block - back) * BLOCK + BLOCK - 1, 0)
            reached = (block >= back) & (ids[end] == ids[block * BLOCK])
            needed = needed + reached.astype(jnp.int32)

        def over(near):
            window = near * BLOCK
            begin = jnp.maximum(block + 1 - near, 0)
            start = pl.multiple_of(begin * BLOCK, BLOCK)
            shape = (BLOCK, BLOCK)
            diagonal = lax.broadcasted_iota(jnp.int32, shape, 0) == lax.broadcasted_iota(
                jnp.int32, shape, 1
            )
            ones = jnp.ones(shape, BF16)
            columns = [
                jnp.dot(
                    jnp.where(diagonal, segment[pl.ds(begin + n, 1), :], 0)
                    .astype(F32).astype(BF16),
                    ones, preferred_element_type=F32,
                )
                for n in range(near)
            ]
            key_at = start + lax.broadcasted_iota(jnp.int32, (window, BLOCK), 0)
            query_at = block * BLOCK + lax.broadcasted_iota(jnp.int32, (window, BLOCK), 1)
            mine = segment[pl.ds(block, 1), :].astype(F32)
            same = jnp.concatenate(columns, axis=0) == mine
            bias = jnp.where(same & (key_at <= query_at), 0.0, -1e30)
            stacked = jnp.concatenate(
                [query[:, h * HEAD_DIM : (h + 1) * HEAD_DIM] for h in range(heads)], axis=0
            )
            scores = lax.dot_general(
                key[pl.ds(start, window), :], stacked, (((1,), (1,)), ((), ())),
                preferred_element_type=F32,
            )
            scores = scores + jnp.concatenate([bias] * heads, axis=1)
            top = jnp.max(scores, axis=0, keepdims=True)
            shifted = jnp.exp2((scores - top) * step)
            inverse = 1.0 / jnp.sum(shifted, axis=0, keepdims=True)
            probs = (shifted * inverse).astype(BF16)
            mixed = lax.dot_general(
                value[pl.ds(start, window), :], probs, (((0,), (0,)), ((), ())),
                preferred_element_type=F32,
            ).astype(BF16)
            for h in range(heads):
                out[0, h * HEAD_DIM : (h + 1) * HEAD_DIM, :] = mixed[:, h * BLOCK : (h + 1) * BLOCK]

        below = 0
        for near in range(2, most + 1):
            fits = (needed <= near) & (needed > below) if near < most else needed > below
            pl.when(fits)(lambda near=near: over(near))
            below = near

        wide = out[0].astype(F32)
        total = jnp.sum(wide * wide, axis=0, keepdims=True)
        square[0] = jnp.broadcast_to(total, (8, BLOCK))
        if weight is not None:
            mat, gain, share = refs[4], refs[5], refs[-1]
            outs = mat.shape[0]
            share[0, 0:outs, :] = jnp.dot(
                mat[...], (wide * gain[...]).astype(BF16), preferred_element_type=F32
            )
            share[0, outs : outs + EXTRA, :] = jnp.broadcast_to(total, (EXTRA, BLOCK))

    in_specs = [
        pl.BlockSpec((BLOCK, width), lambda i, s, d: ((first + i) * 2 + s[0], 0)),
        pl.BlockSpec((length, HEAD_DIM), lambda i, s, d: (0, s[1])),
        pl.BlockSpec((length, HEAD_DIM), lambda i, s, d: (0, s[1])),
        pl.BlockSpec((blocks, BLOCK), lambda i, s, d: (0, 0)),
    ]
    out_specs = [
        pl.BlockSpec((1, width, BLOCK), lambda i, s, d: (i, 0, 0)),
        pl.BlockSpec((1, 8, BLOCK), lambda i, s, d: (i, 0, 0)),
    ]
    out_shape = [
        jax.ShapeDtypeStruct((count, width, BLOCK), BF16),
        jax.ShapeDtypeStruct((count, 8, BLOCK), F32),
    ]
    operands = [query_rows, key_rows, value_rows, segments]
    if weight is not None:
        outs = weight.shape[0]
        in_specs += [
            pl.BlockSpec((outs, width), lambda i, s, d: (0, 0)),
            pl.BlockSpec((width, BLOCK), lambda i, s, d: (0, 0)),
        ]
        operands += [weight, gains]
        out_specs.append(pl.BlockSpec((1, outs + EXTRA, BLOCK), lambda i, s, d: (i, 0, 0)))
        out_shape.append(jax.ShapeDtypeStruct((count, outs + EXTRA, BLOCK), F32))
    grid = pltpu.PrefetchScalarGridSpec(
        num_scalar_prefetch=2, grid=(count,), in_specs=in_specs, out_specs=out_specs
    )
    return pl.pallas_call(body, grid_spec=grid, out_shape=out_shape, name="attention")(
        places, segment_ids, *operands
    )


IN_VMEM = pl.BlockSpec(memory_space=pltpu.VMEM)


def project(attended, squares, weight, gains):
    outs = weight.shape[0]
    rows = outs + EXTRA
    pieces = len(attended)
    count = sum(x.shape[0] for x in attended)

    def body(*refs):
        mat, gain, out = refs[2 * pieces], refs[2 * pieces + 1], refs[-1]
        at = 0
        for att, sq in zip(refs[:pieces], refs[pieces : 2 * pieces]):
            number = att.shape[0]
            wide = jnp.concatenate(
                [(att[u].astype(F32) * gain[...]).astype(BF16) for u in range(number)], axis=1
            )
            sums = jnp.dot(mat[...], wide, preferred_element_type=F32)
            for u in range(number):
                out[at + u, 0:outs, :] = sums[:, u * BLOCK : (u + 1) * BLOCK].astype(BF16)
                out[at + u, outs:rows, :] = scalar_rows(sq[u, 0:1, :])
            at = at + number

    operands = list(attended) + list(squares) + [weight, gains]
    return pl.pallas_call(
        body,
        in_specs=[IN_VMEM] * len(operands),
        out_specs=IN_VMEM,
        out_shape=jax.ShapeDtypeStruct((count, rows, BLOCK), BF16),
        name="project",
    )(*operands)


def together(own, other):
    count, rows, _ = own.shape
    outs = rows - EXTRA

    def body(left, right, out):
        for u in range(count // 2):
            out[u, 0:outs, :] = (
                left[u, 0:outs, :] + right[u, 0:outs, :].astype(F32)
            ).astype(BF16)
            total = left[u, outs : outs + 1, :] + scalar_of(right[u, outs:rows, :])
            out[u, outs:rows, :] = scalar_rows(total)

    spec = pl.BlockSpec((count // 2, rows, BLOCK), lambda i: (i, 0, 0))
    return pl.pallas_call(
        body,
        grid=(2,),
        in_specs=[spec, spec],
        out_specs=spec,
        out_shape=jax.ShapeDtypeStruct(other.shape, BF16),
        name="together",
    )(own, other)


def derive(parts, targets, features, total_tokens):
    count, rows, _ = parts.shape
    outs = rows - EXTRA
    root = math.sqrt(total_tokens)

    def body(got, want, out):
        total = jnp.zeros((1, BLOCK), F32)
        sums = jnp.zeros((outs, BLOCK), F32)
        for u in range(count):
            total = total + scalar_of(got[u, outs:rows, :])
            sums = sums + got[u, 0:outs, :].astype(F32)
        factor = lax.rsqrt(total / features + 1e-06)
        residual = sums * factor - want[...].astype(F32).T
        slope = (jnp.clip(residual, -1.0, 1.0) / root).astype(BF16)
        extra = scalar_rows(factor)
        for u in range(count):
            out[u, 0:outs, :] = slope
            out[u, outs:rows, :] = extra

    return pl.pallas_call(
        body,
        in_specs=[IN_VMEM, IN_VMEM],
        out_specs=IN_VMEM,
        out_shape=jax.ShapeDtypeStruct(parts.shape, BF16),
        name="derive",
    )(parts, targets)


def gradient(slopes, attended, gains, before=None):
    count, rows, _ = slopes.shape
    outs = rows - EXTRA
    width = attended[0].shape[1]

    def body(*refs):
        slope, gain = refs[0], refs[1]
        out = refs[-1]
        normed = []
        for att in refs[2 : 2 + len(attended)]:
            for u in range(att.shape[0]):
                factor = scalar_of(slope[len(normed), outs:rows, :])
                normed.append((att[u].astype(F32) * factor * gain[...]).astype(BF16))
        left = jnp.concatenate([slope[u, 0:outs, :] for u in range(count)], axis=1)
        sums = lax.dot_general(
            left, jnp.concatenate(normed, axis=1), (((1,), (1,)), ((), ())),
            preferred_element_type=F32,
        )
        if before is None:
            out[...] = sums
        else:
            sums = sums + refs[-2][...]
            root = jnp.sqrt(jnp.abs(sums) * ROOT_SCALE)
            out[...] = jnp.where(sums < 0, -root, root)

    operands = [slopes, gains] + list(attended) + ([] if before is None else [before])
    return pl.pallas_call(
        body,
        in_specs=[IN_VMEM] * len(operands),
        out_specs=IN_VMEM,
        out_shape=jax.ShapeDtypeStruct((outs, width), F32),
        name="gradient",
    )(*operands)


def exchange(x, axis, bit):
    size = lax.axis_size(axis)
    return lax.ppermute(x, axis, [(i, i ^ bit) for i in range(size)])


def exchanges(x, low, high):
    return (
        x, exchange(x, "dp", low), exchange(x, "dp", high), exchange(x, "dp", low | high)
    )


def ordered(own, other, axis, bit):
    late = (lax.axis_index(axis) & bit) != 0
    return jnp.where(late, jnp.concatenate([other, own]), jnp.concatenate([own, other]))


def joined(pieces, low, high):
    own, first, second, both = pieces
    return ordered(ordered(own, first, "dp", low), ordered(second, both, "dp", low), "dp", high)


def on_device(query_rows, key_rows, value_rows, segment_ids, norm_gain, draft_weight, targets):
    length, width = query_rows.shape
    blocks = length // BLOCK
    devices = lax.axis_size("tensor")
    total_tokens = length * lax.axis_size("dp")
    place = lax.axis_index("tensor")
    core = place % 2
    chips = [[2 * k + c for k in range(devices // 2)] for c in range(2)]
    kv_head = place * (width // HEAD_DIM) // (HEADS // KV_HEADS)

    segments = segment_ids.reshape(blocks, BLOCK)
    gain = lax.dynamic_slice_in_dim(norm_gain, place * width, width, 0)
    gains = jnp.broadcast_to(gain[:, None], (width, BLOCK))

    def attend(parity, first, count, *more):
        places = jnp.stack([parity, kv_head]).astype(jnp.int32)
        return attention(
            places, segment_ids, first, count, query_rows, key_rows, value_rows, segments, *more
        )

    half = blocks // 2
    cuts = (0, half // 4, half - 3 * half // 8, half)
    round_one = exchanges(draft_weight.T[None], 1, 2)
    theirs_a = attend(1 - core, 0, cuts[1])
    round_one, theirs_a = lax.optimization_barrier((round_one, theirs_a))
    octet = joined(round_one, 1, 2)
    round_two = exchange(octet, "dp", 4)
    theirs_b = attend(1 - core, cuts[1], cuts[2] - cuts[1])
    octet, round_two, theirs_b = lax.optimization_barrier((octet, round_two, theirs_b))
    octet = ordered(octet, round_two, "dp", 4)
    round_three = exchange(octet, "dp", 8)
    theirs_c = attend(1 - core, cuts[2], half - cuts[2])
    octet, round_three, theirs_c = lax.optimization_barrier((octet, round_three, theirs_c))
    weight = ordered(octet, round_three, "dp", 8).reshape(-1, width)

    theirs, squares = zip(theirs_a, theirs_b, theirs_c)
    received = exchange(project(theirs, squares, weight, gains), "tensor", 1)
    mine, _, share = attend(core, 0, half, weight, gains)
    received, share = lax.optimization_barrier((received, share))
    parts = lax.all_to_all(
        together(share, received), "tensor", split_axis=0, concat_axis=0, tiled=True,
        axis_index_groups=chips,
    )
    copies = derive(parts, targets, norm_gain.shape[0], total_tokens)
    my_slopes = lax.all_to_all(
        copies, "tensor", split_axis=0, concat_axis=0, tiled=True, axis_index_groups=chips
    )
    their_slopes = exchange(my_slopes, "tensor", 1)
    partial = gradient(my_slopes, (mine,), gains)
    partial = gradient(their_slopes, theirs, gains, partial)
    shares = partial.reshape(lax.axis_size("dp"), -1, width).astype(F16)
    shares = lax.all_to_all(shares, "dp", split_axis=0, concat_axis=0, tiled=True).astype(F32)
    return jnp.sum(shares * jnp.abs(shares), axis=0).T * (1.0 / ROOT_SCALE)


def solution(mesh):
    placed = (
        P("dp", "tensor"),
        P("dp", None),
        P("dp", None),
        P("dp"),
        P(),
        P("tensor", "dp"),
        P(("dp", "tensor"), None),
    )
    return jax.shard_map(
        on_device, mesh=mesh, in_specs=placed, out_specs=P("tensor", "dp"), check_vma=False
    )
```

time: 415 us -> 133 us (0.32)
  waiting for transfers between devices: 217 us -> 0.29 us
  matrix products: 55 us -> 0 us
  Pallas kernels: 0 us -> 41.3 us
  other arithmetic: 28.6 us -> 3.71 us
  local copies, waits for them, and re-layouts: 20 us -> 4.57 us
  between operations: 13.2 us -> 0.07 us
  starting transfers between devices: 0.08 us -> 11.8 us
  blocking collectives: 74.9 us -> 69.3 us
    reduce_scatter x1 -> x0, waiting for transfers between devices: 149 us -> none  [on_device(): lax.psum_scatter(lax.dot_general(picked, grad_pred, (((0,), (0,)), ((), (...]
    unnamed x4 -> x0, waiting for transfers between devices: 68.1 us -> none
    dot_general x10 -> x0, matrix products: 55 us -> none  [the longest x4 21.1 us: one_block(): jnp.einsum('grqk,kgd->qgrd', probs, values_local, preferred_element_type=...]
    pallas_call x0 -> x9, Pallas kernels: none -> 41.3 us  [the longest x4 25.4 us: attention(): pl.pallas_call(body, grid_spec=grid, out_shape=out_shape, name='attention')]
    all_gather x1 -> x0, blocking collectives: 38.9 us -> none  [on_device(): weight_slab = lax.all_gather(draft_weight, 'dp', axis=1, tiled=True)]
    all_to_all x1 -> x3, blocking collectives: 35.9 us -> 69.3 us  [the longest x1 25.2 us: on_device(): lax.all_to_all(together(share, received), 'tensor', split_axis=0, concat_...]
    reduce_sum x5 -> x1, other arithmetic: 18.4 us -> 0.14 us  [on_device(): return jnp.sum(shares * jnp.abs(shares), axis=0).T * (1.0 / ROOT_SCALE)]
    ppermute x0 -> x7, starting transfers between devices: none -> 11.8 us  [exchange(): return lax.ppermute(x, axis, [(i, i ^ bit) for i in range(size)])]
  transfers between devices with their start and end apart: 3 -> 7, of which waited for: 2 -> 1; matrix products, arithmetic and copies ran while one was open for 21% -> 1% of each run, Pallas kernels for 0% -> 22%
where the time goes in v1:
time: 133 us; the launch traced here: 131 us
  blocking collectives  69.3 us (52%)
  Pallas kernels  41.3 us (31%)
  starting transfers between devices  11.8 us (9%)
  local copies, waits for them, and re-layouts  4.57 us (3%)
  other arithmetic  3.71 us (3%)
    pallas_call x4, Pallas kernels, attention(): pl.pallas_call(body, grid_spec=grid, out_shape=out_shape, name='attention')  25.4 us
    all_to_all x1, blocking collectives, on_device(): lax.all_to_all(together(share, received), 'tensor', split_axis=0, concat_...  25.2 us
    all_to_all x1, blocking collectives, on_device(): lax.all_to_all(shares, 'dp', split_axis=0, concat_axis=0, tiled=True)  23.3 us
    all_to_all x1, blocking collectives, on_device(): lax.all_to_all(copies, 'tensor', split_axis=0, concat_axis=0, tiled=True,...  20.8 us
    ppermute x7, starting transfers between devices, exchange(): return lax.ppermute(x, axis, [(i, i ^ bit) for i in range(size)])  11.8 us
    pallas_call x2, Pallas kernels, gradient(): pl.pallas_call(body, in_specs=[IN_VMEM] * len(operands), out_specs=IN_VME...  7.39 us
    pallas_call x1, Pallas kernels, project(): pl.pallas_call(body, in_specs=[IN_VMEM] * len(operands), out_specs=IN_VME...  3.31 us
    unnamed x8, local copies, waits for them, and re-layouts  2.97 us
  transfers between devices with their start and end apart: 7, of which 1 were waited for; matrix products, arithmetic and copies ran while one was open for 1% of the time, Pallas kernels for 22%

profile of v1, /device:TPU:32, one launch (start us, length us, event | category | flops | bytes accessed | tf_op | source)
XLA Modules:
  0.0 131.0 jit_solution(13683664379792752116)
XLA Ops:
  0.0 1.9 %collective-permute-start.2 = (bf16[1,32,512]{2,1,0:T(8,128)(2,1)}, bf16[1,32,512]{2,1,0:T(8,128)(2,1)S(1)}, u32[]{:S(2)}, u32[]{:S(2)}) collective-permute-start(bf16[1,32,512]{2,1,0:T(8,128)(2,1)} %bitcast.18), channel_id=1, source_target_pairs={{0,48},{16,32},{32,16},{48,0},{64,112},{80,96},{96,80},{112,64},{1... | collective-permute-start | bytes 98312 | tf_op jit(solution)/shard_map/ppermute | solution.py:268
  1.9 2.3 %collective-permute-start.1 = (bf16[1,32,512]{2,1,0:T(8,128)(2,1)}, bf16[1,32,512]{2,1,0:T(8,128)(2,1)S(1)}, u32[]{:S(2)}, u32[]{:S(2)}) collective-permute-start(bf16[1,32,512]{2,1,0:T(8,128)(2,1)} %bitcast.19), channel_id=1, source_target_pairs={{0,32},{16,48},{32,0},{48,16},{64,96},{80,112},{96,64},{112,80},{1... | collective-permute-start | bytes 98312 | tf_op jit(solution)/shard_map/ppermute | solution.py:268
  4.2 0.6 collective-permute-start
  4.7 0.7 pad_add_fusion
  5.4 0.0 copy-start.3
  5.4 4.3 %attention.4 = (bf16[2,512,128]{2,1,0:T(8,128)(2,1)}, f32[2,8,128]{2,1,0:T(8,128)}) custom-call(s32[2]{0:T(128)} %get-tuple-element.53.place, s32[2048]{0:T(1024)} %ids.7, bf16[2048,512]{1,0:T(8,128)(2,1)} %refs_0_.7, bf16[2048,1024]{1,0:T(8,128)(2,1)} %refs_1_.7, bf16[2048,1024]{1,0:T(8,128)(2,1)} %refs_2_.7, s32[16,128]{1,0:T(8,128)} %bitcast.14), custom_call_target="tpu_custom_call" | custom-call | tf_op jit(solution)/shard_map/attention/pallas_call | solution.py:142
  9.7 0.0 collective-permute-done.2
  9.7 0.0 collective-permute-done.1
  9.7 0.0 collective-permute-done
  9.7 0.0 copy-done.3
  9.8 5.1 %collective-permute-start.3 = (bf16[4,32,512]{2,1,0:T(8,128)(2,1)S(1)}, bf16[4,32,512]{2,1,0:T(8,128)(2,1)S(1)}, u32[]{:S(2)}, u32[]{:S(2)}) collective-permute-start(bf16[4,32,512]{2,1,0:T(8,128)(2,1)S(1)} %maximum_select_fusion.2), channel_id=1, source_target_pairs={{0,64},{16,80},{32,96},{48,112},{64,0},{80,16},{96,32},{112,48},{1... | collective-permute-start | bytes 393224 | tf_op jit(solution)/shard_map/ppermute | solution.py:268
  14.9 5.1 %attention.5 = (bf16[3,512,128]{2,1,0:T(8,128)(2,1)}, f32[3,8,128]{2,1,0:T(8,128)}) custom-call(s32[2]{0:T(128)} %get-tuple-element.53.place, s32[2048]{0:T(1024)} %ids.7, bf16[2048,512]{1,0:T(8,128)(2,1)} %refs_0_.7, bf16[2048,1024]{1,0:T(8,128)(2,1)} %refs_1_.7, bf16[2048,1024]{1,0:T(8,128)(2,1)} %refs_2_.7, s32[16,128]{1,0:T(8,128)} %bitcast.15), custom_call_target="tpu_custom_call" | custom-call | tf_op jit(solution)/shard_map/attention/pallas_call | solution.py:142
  20.1 0.3 collective-permute-done.3
  20.4 1.9 %collective-permute-start.4 = (bf16[8,32,512]{2,1,0:T(8,128)(2,1)S(1)}, bf16[8,32,512]{2,1,0:T(8,128)(2,1)S(1)}, u32[]{:S(2)}, u32[]{:S(2)}) collective-permute-start(bf16[8,32,512]{2,1,0:T(8,128)(2,1)S(1)} %maximum_select_fusion.1), channel_id=1, source_target_pairs={{0,128},{16,144},{32,160},{48,176},{64,192},{80,208},{96,224},{112... | collective-permute-start | bytes 786440 | tf_op jit(solution)/shard_map/ppermute | solution.py:268
  22.3 5.0 %attention.6 = (bf16[3,512,128]{2,1,0:T(8,128)(2,1)}, f32[3,8,128]{2,1,0:T(8,128)}) custom-call(s32[2]{0:T(128)} %get-tuple-element.53.place, s32[2048]{0:T(1024)} %ids.7, bf16[2048,512]{1,0:T(8,128)(2,1)} %refs_0_.7, bf16[2048,1024]{1,0:T(8,128)(2,1)} %refs_1_.7, bf16[2048,1024]{1,0:T(8,128)(2,1)} %refs_2_.7, s32[16,128]{1,0:T(8,128)} %bitcast.16), custom_call_target="tpu_custom_call" | custom-call | tf_op jit(solution)/shard_map/attention/pallas_call | solution.py:142
  27.3 0.8 dynamic_slice.3
  28.0 0.0 collective-permute-done.4
  28.0 0.9 maximum_select_fusion
  28.9 0.8 broadcast_in_dim.10.refs_7_.refs_5_.refs_1_
  29.7 3.3 %project.1 = bf16[8,528,128]{2,1,0:T(8,128)(2,1)} custom-call(bf16[2,512,128]{2,1,0:T(8,128)(2,1)} %get-tuple-element.31.refs_0_.refs_2_, bf16[3,512,128]{2,1,0:T(8,128)(2,1)} %get-tuple-element.38.refs_1_.refs_3_, bf16[3,512,128]{2,1,0:T(8,128)(2,1)} %get-tuple-element.43.refs_2_.refs_4_, f32[2,8,128]{2,1,0:T(8,128)} %get-tuple-element.44.refs_3_, ...), custom_call_target="tpu_custom_call" | custom-call | tf_op jit(solution)/shard_map/project/pallas_call | solution.py:171
  33.1 0.0 collective-permute-start.5
  33.1 11.0 %attention.7 = (bf16[8,512,128]{2,1,0:T(8,128)(2,1)}, f32[8,8,128]{2,1,0:T(8,128)}, f32[8,528,128]{2,1,0:T(8,128)}) custom-call(s32[2]{0:T(128)} %get-tuple-element.54.place, s32[2048]{0:T(1024)} %ids.7, bf16[2048,512]{1,0:T(8,128)(2,1)} %refs_0_.7, bf16[2048,1024]{1,0:T(8,128)(2,1)} %refs_1_.7, bf16[2048,1024]{1,0:T(8,128)(2,1)} %refs_2_.7, ...), custom_call_target="tpu_custom_call" | custom-call | tf_op jit(solution)/shard_map/attention/pallas_call | solution.py:142
  44.1 0.0 collective-permute-done.5.right
  44.1 0.0 copy-start.1
  44.1 1.0 copy-done.1
  45.1 2.8 %together.1 = bf16[8,528,128]{2,1,0:T(8,128)(2,1)} custom-call(f32[8,528,128]{2,1,0:T(8,128)} %get-tuple-element.50.left, bf16[8,528,128]{2,1,0:T(8,128)(2,1)} %copy-done.1), custom_call_target="tpu_custom_call" | custom-call | tf_op jit(solution)/shard_map/together/pallas_call | solution.py:193
  47.8 25.2 %all_to_all.15.got = bf16[8,528,128]{2,1,0:T(8,128)(2,1)} all-to-all(bf16[8,528,128]{2,1,0:T(8,128)(2,1)} %together.1), channel_id=1, replica_groups={{0,2,4,6,8,10,12,14},{1,3,5,7,9,11,13,15},{16,18,20,22,24,26,28,30},{17..., dimensions={0} | all-to-all | bytes 2162688 | tf_op jit(solution)/shard_map/all_to_all | solution.py:326
  73.1 2.5 %derive.1 = bf16[8,528,128]{2,1,0:T(8,128)(2,1)} custom-call(bf16[8,528,128]{2,1,0:T(8,128)(2,1)} %all_to_all.15.got, bf16[128,512]{1,0:T(8,128)(2,1)} %want.1), custom_call_target="tpu_custom_call" | custom-call | tf_op jit(solution)/shard_map/derive/pallas_call | solution.py:222
  75.5 20.8 %all_to_all.16.refs_0_ = bf16[8,528,128]{2,1,0:T(8,128)(2,1)S(1)} all-to-all(bf16[8,528,128]{2,1,0:T(8,128)(2,1)} %derive.1), channel_id=1, replica_groups={{0,2,4,6,8,10,12,14},{1,3,5,7,9,11,13,15},{16,18,20,22,24,26,28,30},{17..., dimensions={0} | all-to-all | bytes 2162688 | tf_op jit(solution)/shard_map/all_to_all | solution.py:331
  96.3 0.0 copy-start
  96.3 0.0 collective-permute-start.6
  96.3 1.0 copy-done
  97.3 3.4 %gradient.2.refs_5_ = f32[512,512]{1,0:T(8,128)} custom-call(bf16[8,528,128]{2,1,0:T(8,128)(2,1)} %copy-done, f32[512,128]{1,0:T(8,128)} %broadcast_in_dim.10.refs_7_.refs_5_.refs_1_, bf16[8,512,128]{2,1,0:T(8,128)(2,1)} %get-tuple-element.52.refs_2_), custom_call_target="tpu_custom_call" | custom-call | tf_op jit(solution)/shard_map/gradient/pallas_call | solution.py:257
  100.7 0.0 collective-permute-done.6.refs_0_
  100.7 0.0 copy-start.2
  100.7 1.0 copy-done.2
  101.7 4.0 %gradient.3 = f32[512,512]{1,0:T(8,128)} custom-call(bf16[8,528,128]{2,1,0:T(8,128)(2,1)} %copy-done.2, f32[512,128]{1,0:T(8,128)} %broadcast_in_dim.10.refs_7_.refs_5_.refs_1_, bf16[2,512,128]{2,1,0:T(8,128)(2,1)} %get-tuple-element.31.refs_0_.refs_2_, bf16[3,512,128]{2,1,0:T(8,128)(2,1)} %get-tuple-element.38.refs_1_.refs_3_, ...), custom_call_target="tpu_custom_call" | custom-call | tf_op jit(solution)/shard_map/gradient/pallas_call | solution.py:257
  105.7 1.3 %convert_element_type.9 = f16[512,512]{1,0:T(8,128)(2,1)S(1)} convert(f32[512,512]{1,0:T(8,128)} %gradient.3) | non-fusion elementwise | flops 262144 | bytes 1572864 | tf_op jit(solution)/shard_map/convert_element_type | solution.py:337
  107.0 23.3 %all_to_all.17 = f16[16,32,512]{2,1,0:T(8,128)(2,1)S(1)} all-to-all(f16[16,32,512]{2,1,0:T(8,128)(2,1)S(1)} %bitcast.13), channel_id=1, replica_groups=mesh['dp'=16,'tensor'=16] {'dp'}, dimensions={0} | all-to-all | bytes 1048576 | tf_op jit(solution)/shard_map/all_to_all | solution.py:338
  130.3 0.1 fusion
  130.4 0.6 multiply_bitcast_fusion
  (4 shorter events, 0.1 us)
Async XLA Ops:
  0.0 9.7 %collective-permute-start.2 = (bf16[1,32,512]{2,1,0:T(8,128)(2,1)}, bf16[1,32,512]{2,1,0:T(8,128)(2,1)S(1)}, u32[]{:S(2)}, u32[]{:S(2)}) collective-permute-start(bf16[1,32,512]{2,1,0:T(8,128)(2,1)} %bitcast.18), channel_id=1, source_target_pairs={{0,48},{16,32},{32,16},{48,0},{64,112},{80,96},{96,80},{112,64},{1... | collective-permute-start | bytes 98312 | tf_op jit(solution)/shard_map/ppermute | solution.py:268
  1.9 7.8 %collective-permute-start.1 = (bf16[1,32,512]{2,1,0:T(8,128)(2,1)}, bf16[1,32,512]{2,1,0:T(8,128)(2,1)S(1)}, u32[]{:S(2)}, u32[]{:S(2)}) collective-permute-start(bf16[1,32,512]{2,1,0:T(8,128)(2,1)} %bitcast.19), channel_id=1, source_target_pairs={{0,32},{16,48},{32,0},{48,16},{64,96},{80,112},{96,64},{112,80},{1... | collective-permute-start | bytes 98312 | tf_op jit(solution)/shard_map/ppermute | solution.py:268
  4.2 5.5 %collective-permute-start = (bf16[1,32,512]{2,1,0:T(8,128)(2,1)}, bf16[1,32,512]{2,1,0:T(8,128)(2,1)S(1)}, u32[]{:S(2)}, u32[]{:S(2)}) collective-permute-start(bf16[1,32,512]{2,1,0:T(8,128)(2,1)} %bitcast.20), channel_id=1, source_target_pairs={{0,16},{16,0},{32,48},{48,32},{64,80},{80,64},{96,112},{112,96},{1... | collective-permute-start | bytes 98312 | tf_op jit(solution)/shard_map/ppermute | solution.py:268
  5.4 4.3 %copy-start.3 = (bf16[512,32]{0,1:T(8,128)(2,1)S(1)}, bf16[512,32]{0,1:T(8,128)(2,1)}, u32[]{:S(2)}) copy-start(bf16[512,32]{0,1:T(8,128)(2,1)} %param.12) | copy-start | bytes 98308
  9.8 10.5 %collective-permute-start.3 = (bf16[4,32,512]{2,1,0:T(8,128)(2,1)S(1)}, bf16[4,32,512]{2,1,0:T(8,128)(2,1)S(1)}, u32[]{:S(2)}, u32[]{:S(2)}) collective-permute-start(bf16[4,32,512]{2,1,0:T(8,128)(2,1)S(1)} %maximum_select_fusion.2), channel_id=1, source_target_pairs={{0,64},{16,80},{32,96},{48,112},{64,0},{80,16},{96,32},{112,48},{1... | collective-permute-start | bytes 393224 | tf_op jit(solution)/shard_map/ppermute | solution.py:268
  20.4 7.7 %collective-permute-start.4 = (bf16[8,32,512]{2,1,0:T(8,128)(2,1)S(1)}, bf16[8,32,512]{2,1,0:T(8,128)(2,1)S(1)}, u32[]{:S(2)}, u32[]{:S(2)}) collective-permute-start(bf16[8,32,512]{2,1,0:T(8,128)(2,1)S(1)} %maximum_select_fusion.1), channel_id=1, source_target_pairs={{0,128},{16,144},{32,160},{48,176},{64,192},{80,208},{96,224},{112... | collective-permute-start | bytes 786440 | tf_op jit(solution)/shard_map/ppermute | solution.py:268
  33.1 11.0 %collective-permute-start.5 = (bf16[8,528,128]{2,1,0:T(8,128)(2,1)}, bf16[8,528,128]{2,1,0:T(8,128)(2,1)S(1)}, u32[]{:S(2)}, u32[]{:S(2)}) collective-permute-start(bf16[8,528,128]{2,1,0:T(8,128)(2,1)} %project.1), channel_id=1, source_target_pairs={{0,1},{1,0},{2,3},{3,2},{4,5},{5,4},{6,7},{7,6},{8,9},{9,8},{10,11... | collective-permute-start | bytes 3244040 | tf_op jit(solution)/shard_map/ppermute | solution.py:268
  44.1 1.0 copy-start.1
  96.3 1.0 copy-start
  96.3 4.4 %collective-permute-start.6 = (bf16[8,528,128]{2,1,0:T(8,128)(2,1)S(1)}, bf16[8,528,128]{2,1,0:T(8,128)(2,1)S(1)}, u32[]{:S(2)}, u32[]{:S(2)}) collective-permute-start(bf16[8,528,128]{2,1,0:T(8,128)(2,1)S(1)} %all_to_all.16.refs_0_), channel_id=1, source_target_pairs={{0,1},{1,0},{2,3},{3,2},{4,5},{5,4},{6,7},{7,6},{8,9},{9,8},{10,11... | collective-permute-start | bytes 3244040 | tf_op jit(solution)/shard_map/ppermute | solution.py:268
  100.7 1.0 copy-start.2

commit v2 on v1

--- a/solution.py
+++ b/solution.py
@@ -19,6 +19,14 @@
 ROOT_SCALE = 2.0**20
 
 
+ROOM = pltpu.CompilerParams(vmem_limit_bytes=24 << 20)
+IN_VMEM = pl.BlockSpec(memory_space=pltpu.VMEM)
+
+
+def in_vmem(*arrays):
+    return [pltpu.with_memory_space_constraint(x, pltpu.VMEM) for x in arrays]
+
+
 def scalar_rows(x):
     rows = lax.broadcasted_iota(jnp.int32, (EXTRA, BLOCK), 0)
     high = x.astype(BF16).astype(F32)
@@ -35,7 +43,7 @@
 
 
 def attention(
-    places, segment_ids, first, count, query_rows, key_rows, value_rows, segments,
+    places, segment_ids, first, count, query_rows, keys, values, segments,
     weight=None, gains=None,
 ):
     length, width = query_rows.shape
@@ -47,7 +55,8 @@
     def body(place, ids, *refs):
         query, key, value, segment = refs[:4]
         out, square = refs[-2:] if weight is None else refs[-3:-1]
-        block = (first + pl.program_id(0)) * 2 + place[0]
+        at = pl.program_id(0)
+        block = (first + at) * 2 + place[0]
         needed = 1
         for back in range(1, most):
             end = jnp.maximum((block - back) * BLOCK + BLOCK - 1, 0)
@@ -93,7 +102,7 @@
                 preferred_element_type=F32,
             ).astype(BF16)
             for h in range(heads):
-                out[0, h * HEAD_DIM : (h + 1) * HEAD_DIM, :] = mixed[:, h * BLOCK : (h + 1) * BLOCK]
+                out[at, h * HEAD_DIM : (h + 1) * HEAD_DIM, :] = mixed[:, h * BLOCK : (h + 1) * BLOCK]
 
         below = 0
         for near in range(2, most + 1):
@@ -101,50 +110,37 @@
             pl.when(fits)(lambda near=near: over(near))
             below = near
 
-        wide = out[0].astype(F32)
+        wide = out[at].astype(F32)
         total = jnp.sum(wide * wide, axis=0, keepdims=True)
-        square[0] = jnp.broadcast_to(total, (8, BLOCK))
+        square[at] = jnp.broadcast_to(total, (8, BLOCK))
         if weight is not None:
             mat, gain, share = refs[4], refs[5], refs[-1]
             outs = mat.shape[0]
-            share[0, 0:outs, :] = jnp.dot(
+            share[at, 0:outs, :] = jnp.dot(
                 mat[...], (wide * gain[...]).astype(BF16), preferred_element_type=F32
             )
-            share[0, outs : outs + EXTRA, :] = jnp.broadcast_to(total, (EXTRA, BLOCK))
-
-    in_specs = [
-        pl.BlockSpec((BLOCK, width), lambda i, s, d: ((first + i) * 2 + s[0], 0)),
-        pl.BlockSpec((length, HEAD_DIM), lambda i, s, d: (0, s[1])),
-        pl.BlockSpec((length, HEAD_DIM), lambda i, s, d: (0, s[1])),
-        pl.BlockSpec((blocks, BLOCK), lambda i, s, d: (0, 0)),
+            share[at, outs : outs + EXTRA, :] = jnp.broadcast_to(total, (EXTRA, BLOCK))
+
+    in_specs = [pl.BlockSpec((BLOCK, width), lambda i, s, d: ((first + i) * 2 + s[0], 0))]
+    out_shape = [
+        pltpu.VMEM((count, width, BLOCK), BF16),
+        pltpu.VMEM((count, 8, BLOCK), F32),
     ]
-    out_specs = [
-        pl.BlockSpec((1, width, BLOCK), lambda i, s, d: (i, 0, 0)),
-        pl.BlockSpec((1, 8, BLOCK), lambda i, s, d: (i, 0, 0)),
-    ]
-    out_shape = [
-        jax.ShapeDtypeStruct((count, width, BLOCK), BF16),
-        jax.ShapeDtypeStruct((count, 8, BLOCK), F32),
-    ]
-    operands = [query_rows, key_rows, value_rows, segments]
+    operands = [query_rows, *in_vmem(keys, values), segments]
     if weight is not None:
-        outs = weight.shape[0]
-        in_specs += [
-            pl.BlockSpec((outs, width), lambda i, s, d: (0, 0)),
-            pl.BlockSpec((width, BLOCK), lambda i, s, d: (0, 0)),
-        ]
-        operands += [weight, gains]
-        out_specs.append(pl.BlockSpec((1, outs + EXTRA, BLOCK), lambda i, s, d: (i, 0, 0)))
-        out_shape.append(jax.ShapeDtypeStruct((count, outs + EXTRA, BLOCK), F32))
+        operands += in_vmem(weight, gains)
+        out_shape.append(pltpu.VMEM((count, weight.shape[0] + EXTRA, BLOCK), F32))
     grid = pltpu.PrefetchScalarGridSpec(
-        num_scalar_prefetch=2, grid=(count,), in_specs=in_specs, out_specs=out_specs
-    )
-    return pl.pallas_call(body, grid_spec=grid, out_shape=out_shape, name="attention")(
+        num_scalar_prefetch=2,
+        grid=(count,),
+        in_specs=in_specs + [IN_VMEM] * (len(operands) - 1),
+        out_specs=[IN_VMEM] * len(out_shape),
+    )
+    return pl.pallas_call(body, grid_spec=grid, out_shape=out_shape, name="attention",
+        compiler_params=ROOM,
+    )(
         places, segment_ids, *operands
     )
-
-
-IN_VMEM = pl.BlockSpec(memory_space=pltpu.VMEM)
 
 
 def project(attended, squares, weight, gains):
@@ -172,9 +168,10 @@
         body,
         in_specs=[IN_VMEM] * len(operands),
         out_specs=IN_VMEM,
-        out_shape=jax.ShapeDtypeStruct((count, rows, BLOCK), BF16),
+        out_shape=pltpu.VMEM((count, rows, BLOCK), BF16),
         name="project",
-    )(*operands)
+        compiler_params=ROOM,
+    )(*in_vmem(*operands))
 
 
 def together(own, other):
@@ -182,22 +179,21 @@
     outs = rows - EXTRA
 
     def body(left, right, out):
-        for u in range(count // 2):
+        for u in range(count):
             out[u, 0:outs, :] = (
                 left[u, 0:outs, :] + right[u, 0:outs, :].astype(F32)
             ).astype(BF16)
             total = left[u, outs : outs + 1, :] + scalar_of(right[u, outs:rows, :])
             out[u, outs:rows, :] = scalar_rows(total)
 
-    spec = pl.BlockSpec((count // 2, rows, BLOCK), lambda i: (i, 0, 0))
     return pl.pallas_call(
         body,
-        grid=(2,),
-        in_specs=[spec, spec],
-        out_specs=spec,
-        out_shape=jax.ShapeDtypeStruct(other.shape, BF16),
+        in_specs=[IN_VMEM, IN_VMEM],
+        out_specs=IN_VMEM,
+        out_shape=pltpu.VMEM(other.shape, BF16),
         name="together",
-    )(own, other)
+        compiler_params=ROOM,
+    )(*in_vmem(own, other))
 
 
 def derive(parts, targets, features, total_tokens):
@@ -223,9 +219,10 @@
         body,
         in_specs=[IN_VMEM, IN_VMEM],
         out_specs=IN_VMEM,
-        out_shape=jax.ShapeDtypeStruct(parts.shape, BF16),
+        out_shape=pltpu.VMEM(parts.shape, BF16),
         name="derive",
-    )(parts, targets)
+        compiler_params=ROOM,
+    )(*in_vmem(parts, targets))
 
 
 def gradient(slopes, attended, gains, before=None):
@@ -258,9 +255,10 @@
         body,
         in_specs=[IN_VMEM] * len(operands),
         out_specs=IN_VMEM,
-        out_shape=jax.ShapeDtypeStruct((outs, width), F32),
+        out_shape=pltpu.VMEM((outs, width), F32),
         name="gradient",
-    )(*operands)
+        compiler_params=ROOM,
+    )(*in_vmem(*operands))
 
 
 def exchange(x, axis, bit):
@@ -295,13 +293,15 @@
     kv_head = place * (width // HEAD_DIM) // (HEADS // KV_HEADS)
 
     segments = segment_ids.reshape(blocks, BLOCK)
+    keys = lax.dynamic_slice_in_dim(key_rows, kv_head * HEAD_DIM, HEAD_DIM, 1)
+    values = lax.dynamic_slice_in_dim(value_rows, kv_head * HEAD_DIM, HEAD_DIM, 1)
     gain = lax.dynamic_slice_in_dim(norm_gain, place * width, width, 0)
     gains = jnp.broadcast_to(gain[:, None], (width, BLOCK))
 
     def attend(parity, first, count, *more):
-        places = jnp.stack([parity, kv_head]).astype(jnp.int32)
+        places = parity.astype(jnp.int32).reshape(1)
         return attention(
-            places, segment_ids, first, count, query_rows, key_rows, value_rows, segments, *more
+            places, segment_ids, first, count, query_rows, keys, values, segments, *more
         )
 
     half = blocks // 2

time: 133 us -> 117 us (0.88); the launches traced: 131 us -> 117 us
  Pallas kernels: 41.3 us -> 20.5 us
  waiting for transfers between devices: 0.29 us -> 3.73 us
  other arithmetic: 3.71 us -> 5.55 us
    pallas_call x5, Pallas kernels: 28.2 us -> 17.6 us  [the longest x4 17.4 us: attention(): pl.pallas_call(body, grid_spec=grid, out_shape=out_shape, name='attention...]
    pallas_call x2, Pallas kernels: 7.39 us -> 1.84 us  [gradient(): pl.pallas_call(body, in_specs=[IN_VMEM] * len(operands), out_specs=IN_VME...]
    select_n x5, other arithmetic: 0.95 us -> 4.67 us  [ordered(): jnp.where(late, jnp.concatenate([other, own]), jnp.concatenate([own, othe...]
    ppermute x7, waiting for transfers between devices: 0.29 us -> 3.73 us  [exchange(): return lax.ppermute(x, axis, [(i, i ^ bit) for i in range(size)])]
    pallas_call x1, Pallas kernels: 3.31 us -> 0.86 us  [project(): pl.pallas_call(body, in_specs=[IN_VMEM] * len(operands), out_specs=IN_VME...]
    pallas_call x1, Pallas kernels: 2.46 us -> 0.21 us  [derive(): pl.pallas_call(body, in_specs=[IN_VMEM, IN_VMEM], out_specs=IN_VMEM, out_...]
    dynamic_slice x0 -> x1, local copies, waits for them, and re-layouts: none -> 1.43 us  [on_device(): lax.dynamic_slice_in_dim(value_rows, kv_head * HEAD_DIM, HEAD_DIM, 1)]
    unnamed x8 -> x26, local copies, waits for them, and re-layouts: 2.97 us -> 3.09 us
  transfers between devices with their start and end apart: 7 -> 7, of which waited for: 1 -> 2; matrix products, arithmetic and copies ran while one was open for 1% -> 2% of each run, Pallas kernels for 22% -> 16%
where the time goes in v2:
time: 117 us
  blocking collectives  70.1 us (60%)
  Pallas kernels  20.5 us (18%)
  starting transfers between devices  11.6 us (10%)
  other arithmetic  5.55 us (5%)
  local copies, waits for them, and re-layouts  5.48 us (5%)
  waiting for transfers between devices  3.73 us (3%)
    all_to_all x1, blocking collectives, on_device(): lax.all_to_all(together(share, received), 'tensor', split_axis=0, concat_...  25.7 us
    all_to_all x1, blocking collectives, on_device(): lax.all_to_all(shares, 'dp', split_axis=0, concat_axis=0, tiled=True)  23.9 us
    all_to_all x1, blocking collectives, on_device(): lax.all_to_all(copies, 'tensor', split_axis=0, concat_axis=0, tiled=True,...  20.4 us
    pallas_call x4, Pallas kernels, attention(): pl.pallas_call(body, grid_spec=grid, out_shape=out_shape, name='attention...  17.4 us
    ppermute x7, starting transfers between devices, exchange(): return lax.ppermute(x, axis, [(i, i ^ bit) for i in range(size)])  11.6 us
    select_n x5, other arithmetic, ordered(): jnp.where(late, jnp.concatenate([other, own]), jnp.concatenate([own, othe...  4.67 us
    ppermute x7, waiting for transfers between devices, exchange(): return lax.ppermute(x, axis, [(i, i ^ bit) for i in range(size)])  3.73 us
    unnamed x26, local copies, waits for them, and re-layouts  3.09 us
  transfers between devices with their start and end apart: 7, of which 2 were waited for; matrix products, arithmetic and copies ran while one was open for 2% of the time, Pallas kernels for 16%

profile of v2, /device:TPU:32, one launch (start us, length us, event | category | flops | bytes accessed | tf_op | source)
XLA Modules:
  0.0 117.1 jit_solution(11252775672143771482)
XLA Ops:
  0.0 1.8 %collective-permute-start = (bf16[1,32,512]{2,1,0:T(8,128)(2,1)}, bf16[1,32,512]{2,1,0:T(8,128)(2,1)S(1)}, u32[]{:S(2)}, u32[]{:S(2)}) collective-permute-start(bf16[1,32,512]{2,1,0:T(8,128)(2,1)} %bitcast.17), channel_id=1, source_target_pairs={{0,16},{16,0},{32,48},{48,32},{64,80},{80,64},{96,112},{112,96},{1... | collective-permute-start | bytes 98312 | tf_op jit(solution)/shard_map/ppermute | solution.py:266
  1.8 1.6 %collective-permute-start.1 = (bf16[1,32,512]{2,1,0:T(8,128)(2,1)}, bf16[1,32,512]{2,1,0:T(8,128)(2,1)S(1)}, u32[]{:S(2)}, u32[]{:S(2)}) collective-permute-start(bf16[1,32,512]{2,1,0:T(8,128)(2,1)} %bitcast.18), channel_id=1, source_target_pairs={{0,32},{16,48},{32,0},{48,16},{64,96},{80,112},{96,64},{112,80},{1... | collective-permute-start | bytes 98312 | tf_op jit(solution)/shard_map/ppermute | solution.py:266
  3.4 0.5 collective-permute-start.2
  3.8 1.4 %constant_dynamic-slice_fusion = (bf16[2048,128]{1,0:T(8,128)(2,1)S(1)}, bf16[2048,128]{1,0:T(8,128)(2,1)S(1)}) fusion(bf16[2048,1024]{1,0:T(8,128)(2,1)} %param.9, s32[]{:T(128)S(6)} %select_n.60, bf16[2048,1024]{1,0:T(8,128)(2,1)} %param.8), kind=kLoop, calls=%fused_computation.8 | loop fusion | bytes 2097156 | tf_op jit(solution)/shard_map/dynamic_slice | solution.py:297
  5.3 0.5 copy-done
  5.8 0.0 copy-done.5
  5.8 2.1 %attention.4 = (bf16[2,512,128]{2,1,0:T(8,128)(2,1)S(1)}, f32[2,8,128]{2,1,0:T(8,128)S(1)}) custom-call(s32[1]{0:T(128)} %bitcast.3.place, s32[2048]{0:T(1024)S(1)} %copy-done.5, bf16[2048,512]{1,0:T(8,128)(2,1)S(1)} %copy-done, bf16[2048,128]{1,0:T(8,128)(2,1)S(1)} %get-tuple-element.54.refs_1_, bf16[2048,128]{1,0:T(8,128)(2,1)S(1)} %get-tuple-element.53.refs_2_, ...), custom_call_target="tpu_custom_call" | custom-call | tf_op jit(solution)/shard_map/attention/pallas_call | solution.py:139
  7.9 0.0 copy-start.3
  7.9 0.0 collective-permute-done
  7.9 0.0 collective-permute-done.1
  7.9 0.0 copy-start.12
  7.9 0.0 collective-permute-done.2
  8.0 0.6 copy-done.12
  8.6 0.8 maximum_select_fusion.3
  9.5 0.0 copy-done.11
  9.5 0.7 maximum_select_fusion.2
  10.2 0.0 copy-done.3
  10.2 5.9 %collective-permute-start.3 = (bf16[4,32,512]{2,1,0:T(8,128)(2,1)}, bf16[4,32,512]{2,1,0:T(8,128)(2,1)}, u32[]{:S(2)}, u32[]{:S(2)}) collective-permute-start(bf16[4,32,512]{2,1,0:T(8,128)(2,1)} %maximum_select_fusion.2), channel_id=1, source_target_pairs={{0,64},{16,80},{32,96},{48,112},{64,0},{80,16},{96,32},{112,48},{1... | collective-permute-start | bytes 393224 | tf_op jit(solution)/shard_map/ppermute | solution.py:266
  16.1 3.2 %attention.5 = (bf16[3,512,128]{2,1,0:T(8,128)(2,1)S(1)}, f32[3,8,128]{2,1,0:T(8,128)S(1)}) custom-call(s32[1]{0:T(128)} %bitcast.3.place, s32[2048]{0:T(1024)S(1)} %copy-done.5, bf16[2048,512]{1,0:T(8,128)(2,1)S(1)} %copy-done, bf16[2048,128]{1,0:T(8,128)(2,1)S(1)} %get-tuple-element.54.refs_1_, bf16[2048,128]{1,0:T(8,128)(2,1)S(1)} %get-tuple-element.53.refs_2_, ...), custom_call_target="tpu_custom_call" | custom-call | tf_op jit(solution)/shard_map/attention/pallas_call | solution.py:139
  19.3 0.0 copy-start.7
  19.4 0.6 copy-done.7
  19.9 1.8 %collective-permute-done.3 = bf16[4,32,512]{2,1,0:T(8,128)(2,1)} collective-permute-done((bf16[4,32,512]{2,1,0:T(8,128)(2,1)}, bf16[4,32,512]{2,1,0:T(8,128)(2,1)}, u32[]{:S(2)}, u32[]{:S(2)}) %collective-permute-start.3) | collective-permute-done | bytes 131104 | tf_op jit(solution)/shard_map/ppermute | solution.py:266
  21.7 1.9 %maximum_select_fusion.1 = bf16[8,32,512]{2,1,0:T(8,128)(2,1)} fusion(bf16[4,32,512]{2,1,0:T(8,128)(2,1)} %maximum_select_fusion.2, bf16[4,32,512]{2,1,0:T(8,128)(2,1)} %collective-permute-done.3, pred[]{:T(512)S(6)} %ne.32), kind=kLoop, calls=%fused_computation.3 | loop fusion | flops 393216 | bytes 524289 | tf_op jit(solution)/shard_map/jit(_where)/select_n | solution.py:277
  23.6 1.5 %collective-permute-start.4 = (bf16[8,32,512]{2,1,0:T(8,128)(2,1)}, bf16[8,32,512]{2,1,0:T(8,128)(2,1)}, u32[]{:S(2)}, u32[]{:S(2)}) collective-permute-start(bf16[8,32,512]{2,1,0:T(8,128)(2,1)} %maximum_select_fusion.1), channel_id=1, source_target_pairs={{0,128},{16,144},{32,160},{48,176},{64,192},{80,208},{96,224},{112... | collective-permute-start | bytes 786440 | tf_op jit(solution)/shard_map/ppermute | solution.py:266
  25.1 3.1 %attention.6 = (bf16[3,512,128]{2,1,0:T(8,128)(2,1)S(1)}, f32[3,8,128]{2,1,0:T(8,128)S(1)}) custom-call(s32[1]{0:T(128)} %bitcast.3.place, s32[2048]{0:T(1024)S(1)} %copy-done.5, bf16[2048,512]{1,0:T(8,128)(2,1)S(1)} %copy-done, bf16[2048,128]{1,0:T(8,128)(2,1)S(1)} %get-tuple-element.54.refs_1_, bf16[2048,128]{1,0:T(8,128)(2,1)S(1)} %get-tuple-element.53.refs_2_, ...), custom_call_target="tpu_custom_call" | custom-call | tf_op jit(solution)/shard_map/attention/pallas_call | solution.py:139
  28.2 0.0 copy-start.1
  28.2 0.7 copy-done.1
  29.0 0.6 copy-done.9
  29.6 0.8 dynamic_slice.11
  30.4 0.0 collective-permute-done.4
  30.4 1.3 %maximum_select_fusion = bf16[16,32,512]{2,1,0:T(8,128)(2,1)S(1)} fusion(bf16[8,32,512]{2,1,0:T(8,128)(2,1)} %maximum_select_fusion.1, bf16[8,32,512]{2,1,0:T(8,128)(2,1)} %collective-permute-done.4, pred[]{:T(512)S(6)} %ne.33), kind=kLoop, calls=%fused_computation.2 | loop fusion | flops 786432 | bytes 1048577 | tf_op jit(solution)/shard_map/jit(_where)/select_n | solution.py:277
  31.7 0.1 broadcast_in_dim.10.refs_7_.refs_5_.refs_1_
  31.9 0.9 project.1
  32.7 0.3 collective-permute-start.5
  33.0 8.9 %attention.7 = (bf16[8,512,128]{2,1,0:T(8,128)(2,1)S(1)}, f32[8,8,128]{2,1,0:T(8,128)}, f32[8,528,128]{2,1,0:T(8,128)S(1)}) custom-call(s32[1]{0:T(128)} %bitcast.6.place, s32[2048]{0:T(1024)S(1)} %copy-done.5, bf16[2048,512]{1,0:T(8,128)(2,1)S(1)} %copy-done, bf16[2048,128]{1,0:T(8,128)(2,1)S(1)} %get-tuple-element.54.refs_1_, ...), custom_call_target="tpu_custom_call" | custom-call | tf_op jit(solution)/shard_map/attention/pallas_call | solution.py:139
  41.9 0.0 collective-permute-done.5.right
  41.9 0.2 together.1
  42.1 25.7 %all_to_all.15.got = bf16[8,528,128]{2,1,0:T(8,128)(2,1)S(1)} all-to-all(bf16[8,528,128]{2,1,0:T(8,128)(2,1)S(1)} %together.1), channel_id=1, replica_groups={{0,2,4,6,8,10,12,14},{1,3,5,7,9,11,13,15},{16,18,20,22,24,26,28,30},{17..., dimensions={0} | all-to-all | bytes 2162688 | tf_op jit(solution)/shard_map/all_to_all | solution.py:326
  67.9 0.2 derive.1
  68.1 20.4 %all_to_all.16.refs_0_ = bf16[8,528,128]{2,1,0:T(8,128)(2,1)S(1)} all-to-all(bf16[8,528,128]{2,1,0:T(8,128)(2,1)S(1)} %derive.1), channel_id=1, replica_groups={{0,2,4,6,8,10,12,14},{1,3,5,7,9,11,13,15},{16,18,20,22,24,26,28,30},{17..., dimensions={0} | all-to-all | bytes 2162688 | tf_op jit(solution)/shard_map/all_to_all | solution.py:331
  88.5 0.0 collective-permute-start.6
  88.5 0.8 gradient.2.refs_5_
  89.3 1.9 %collective-permute-done.6.refs_0_ = bf16[8,528,128]{2,1,0:T(8,128)(2,1)S(1)} collective-permute-done((bf16[8,528,128]{2,1,0:T(8,128)(2,1)S(1)}, bf16[8,528,128]{2,1,0:T(8,128)(2,1)S(1)}, u32[]{:S(2)}, u32[]{:S(2)}) %collective-permute-start.6) | collective-permute-done | bytes 1081376 | tf_op jit(solution)/shard_map/ppermute | solution.py:266
  91.2 1.1 gradient.3
  92.3 0.1 convert_element_type.9
  92.4 23.9 %all_to_all.17 = f16[16,32,512]{2,1,0:T(8,128)(2,1)S(1)} all-to-all(f16[16,32,512]{2,1,0:T(8,128)(2,1)S(1)} %bitcast.16), channel_id=1, replica_groups=mesh['dp'=16,'tensor'=16] {'dp'}, dimensions={0} | all-to-all | bytes 1048576 | tf_op jit(solution)/shard_map/all_to_all | solution.py:338
  116.3 0.1 fusion
  116.5 0.6 multiply_bitcast_fusion
  (15 shorter events, 0.0 us)
Async XLA Ops:
  0.0 7.9 %collective-permute-start = (bf16[1,32,512]{2,1,0:T(8,128)(2,1)}, bf16[1,32,512]{2,1,0:T(8,128)(2,1)S(1)}, u32[]{:S(2)}, u32[]{:S(2)}) collective-permute-start(bf16[1,32,512]{2,1,0:T(8,128)(2,1)} %bitcast.17), channel_id=1, source_target_pairs={{0,16},{16,0},{32,48},{48,32},{64,80},{80,64},{96,112},{112,96},{1... | collective-permute-start | bytes 98312 | tf_op jit(solution)/shard_map/ppermute | solution.py:266
  1.8 6.1 %collective-permute-start.1 = (bf16[1,32,512]{2,1,0:T(8,128)(2,1)}, bf16[1,32,512]{2,1,0:T(8,128)(2,1)S(1)}, u32[]{:S(2)}, u32[]{:S(2)}) collective-permute-start(bf16[1,32,512]{2,1,0:T(8,128)(2,1)} %bitcast.18), channel_id=1, source_target_pairs={{0,32},{16,48},{32,0},{48,16},{64,96},{80,112},{96,64},{112,80},{1... | collective-permute-start | bytes 98312 | tf_op jit(solution)/shard_map/ppermute | solution.py:266
  3.4 4.6 %collective-permute-start.2 = (bf16[1,32,512]{2,1,0:T(8,128)(2,1)}, bf16[1,32,512]{2,1,0:T(8,128)(2,1)}, u32[]{:S(2)}, u32[]{:S(2)}) collective-permute-start(bf16[1,32,512]{2,1,0:T(8,128)(2,1)} %bitcast.19), channel_id=1, source_target_pairs={{0,48},{16,32},{32,16},{48,0},{64,112},{80,96},{96,80},{112,64},{1... | collective-permute-start | bytes 98312 | tf_op jit(solution)/shard_map/ppermute | solution.py:266
  3.8 1.9 %copy-start = (bf16[2048,512]{1,0:T(8,128)(2,1)S(1)}, bf16[2048,512]{1,0:T(8,128)(2,1)}, u32[]{:S(2)}) copy-start(bf16[2048,512]{1,0:T(8,128)(2,1)} %refs_0_.7) | copy-start | bytes 6291460
  3.8 1.9 %copy-start.5 = (s32[2048]{0:T(1024)S(1)}, s32[2048]{0:T(1024)}, u32[]{:S(2)}) copy-start(s32[2048]{0:T(1024)} %ids.7) | copy-start | bytes 24580
  5.8 3.7 %copy-start.11 = (bf16[512,32]{0,1:T(8,128)(2,1)S(1)}, bf16[512,32]{0,1:T(8,128)(2,1)}, u32[]{:S(2)}) copy-start(bf16[512,32]{0,1:T(8,128)(2,1)} %param.12) | copy-start | bytes 98308
  7.9 2.3 %copy-start.3 = (bf16[2,512,128]{2,1,0:T(8,128)(2,1)}, bf16[2,512,128]{2,1,0:T(8,128)(2,1)S(1)}, u32[]{:S(2)}) copy-start(bf16[2,512,128]{2,1,0:T(8,128)(2,1)S(1)} %get-tuple-element.31.refs_0_.refs_2_) | copy-start | bytes 786436
  7.9 0.7 copy-start.12
  10.2 11.6 %collective-permute-start.3 = (bf16[4,32,512]{2,1,0:T(8,128)(2,1)}, bf16[4,32,512]{2,1,0:T(8,128)(2,1)}, u32[]{:S(2)}, u32[]{:S(2)}) collective-permute-start(bf16[4,32,512]{2,1,0:T(8,128)(2,1)} %maximum_select_fusion.2), channel_id=1, source_target_pairs={{0,64},{16,80},{32,96},{48,112},{64,0},{80,16},{96,32},{112,48},{1... | collective-permute-start | bytes 393224 | tf_op jit(solution)/shard_map/ppermute | solution.py:266
  19.3 0.6 copy-start.7
  23.6 6.8 %collective-permute-start.4 = (bf16[8,32,512]{2,1,0:T(8,128)(2,1)}, bf16[8,32,512]{2,1,0:T(8,128)(2,1)}, u32[]{:S(2)}, u32[]{:S(2)}) collective-permute-start(bf16[8,32,512]{2,1,0:T(8,128)(2,1)} %maximum_select_fusion.1), channel_id=1, source_target_pairs={{0,128},{16,144},{32,160},{48,176},{64,192},{80,208},{96,224},{112... | collective-permute-start | bytes 786440 | tf_op jit(solution)/shard_map/ppermute | solution.py:266
  28.2 0.8 copy-start.1
  29.0 0.6 copy-start.9
  29.6 2.2 %copy-start.2 = (bf16[3,512,128]{2,1,0:T(8,128)(2,1)S(1)}, bf16[3,512,128]{2,1,0:T(8,128)(2,1)}, u32[]{:S(2)}) copy-start(bf16[3,512,128]{2,1,0:T(8,128)(2,1)} %copy-done.1) | copy-start | bytes 1179652
  29.6 2.3 %copy-start.4 = (bf16[2,512,128]{2,1,0:T(8,128)(2,1)S(1)}, bf16[2,512,128]{2,1,0:T(8,128)(2,1)}, u32[]{:S(2)}) copy-start(bf16[2,512,128]{2,1,0:T(8,128)(2,1)} %copy-done.3) | copy-start | bytes 786436
  29.6 2.3 %copy-start.8 = (f32[3,8,128]{2,1,0:T(8,128)S(1)}, f32[3,8,128]{2,1,0:T(8,128)}, u32[]{:S(2)}) copy-start(f32[3,8,128]{2,1,0:T(8,128)} %copy-done.7) | copy-start | bytes 36868
  29.6 2.3 %copy-start.10 = (f32[3,8,128]{2,1,0:T(8,128)S(1)}, f32[3,8,128]{2,1,0:T(8,128)}, u32[]{:S(2)}) copy-start(f32[3,8,128]{2,1,0:T(8,128)} %copy-done.9) | copy-start | bytes 36868
  32.7 9.2 %collective-permute-start.5 = (bf16[8,528,128]{2,1,0:T(8,128)(2,1)S(1)}, bf16[8,528,128]{2,1,0:T(8,128)(2,1)S(1)}, u32[]{:S(2)}, u32[]{:S(2)}) collective-permute-start(bf16[8,528,128]{2,1,0:T(8,128)(2,1)S(1)} %project.1), channel_id=1, source_target_pairs={{0,1},{1,0},{2,3},{3,2},{4,5},{5,4},{6,7},{7,6},{8,9},{9,8},{10,11... | collective-permute-start | bytes 3244040 | tf_op jit(solution)/shard_map/ppermute | solution.py:266
  42.1 25.7 %copy-start.6 = (bf16[128,512]{1,0:T(8,128)(2,1)S(1)}, bf16[128,512]{1,0:T(8,128)(2,1)}, u32[]{:S(2)}) copy-start(bf16[128,512]{1,0:T(8,128)(2,1)} %want.1) | copy-start | bytes 393220
  88.5 2.7 %collective-permute-start.6 = (bf16[8,528,128]{2,1,0:T(8,128)(2,1)S(1)}, bf16[8,528,128]{2,1,0:T(8,128)(2,1)S(1)}, u32[]{:S(2)}, u32[]{:S(2)}) collective-permute-start(bf16[8,528,128]{2,1,0:T(8,128)(2,1)S(1)} %all_to_all.16.refs_0_), channel_id=1, source_target_pairs={{0,1},{1,0},{2,3},{3,2},{4,5},{5,4},{6,7},{7,6},{8,9},{9,8},{10,11... | collective-permute-start | bytes 3244040 | tf_op jit(solution)/shard_map/ppermute | solution.py:266

commit v3 on v2

--- a/solution.py
+++ b/solution.py
@@ -43,8 +43,7 @@
 
 
 def attention(
-    places, segment_ids, first, count, query_rows, keys, values, segments,
-    weight=None, gains=None,
+    places, segment_ids, first, count, query_rows, keys, values, segments
 ):
     length, width = query_rows.shape
     heads = width // HEAD_DIM
@@ -54,7 +53,7 @@
 
     def body(place, ids, *refs):
         query, key, value, segment = refs[:4]
-        out, square = refs[-2:] if weight is None else refs[-3:-1]
+        out, square = refs[-2:]
         at = pl.program_id(0)
         block = (first + at) * 2 + place[0]
         needed = 1
@@ -113,13 +112,6 @@
         wide = out[at].astype(F32)
         total = jnp.sum(wide * wide, axis=0, keepdims=True)
         square[at] = jnp.broadcast_to(total, (8, BLOCK))
-        if weight is not None:
-            mat, gain, share = refs[4], refs[5], refs[-1]
-            outs = mat.shape[0]
-            share[at, 0:outs, :] = jnp.dot(
-                mat[...], (wide * gain[...]).astype(BF16), preferred_element_type=F32
-            )
-            share[at, outs : outs + EXTRA, :] = jnp.broadcast_to(total, (EXTRA, BLOCK))
 
     in_specs = [pl.BlockSpec((BLOCK, width), lambda i, s, d: ((first + i) * 2 + s[0], 0))]
     out_shape = [
@@ -127,9 +119,6 @@
         pltpu.VMEM((count, 8, BLOCK), F32),
     ]
     operands = [query_rows, *in_vmem(keys, values), segments]
-    if weight is not None:
-        operands += in_vmem(weight, gains)
-        out_shape.append(pltpu.VMEM((count, weight.shape[0] + EXTRA, BLOCK), F32))
     grid = pltpu.PrefetchScalarGridSpec(
         num_scalar_prefetch=2,
         grid=(count,),
@@ -143,7 +132,7 @@
     )
 
 
-def project(attended, squares, weight, gains):
+def project(attended, squares, weight, gains, kind):
     outs = weight.shape[0]
     rows = outs + EXTRA
     pieces = len(attended)
@@ -159,8 +148,11 @@
             )
             sums = jnp.dot(mat[...], wide, preferred_element_type=F32)
             for u in range(number):
-                out[at + u, 0:outs, :] = sums[:, u * BLOCK : (u + 1) * BLOCK].astype(BF16)
-                out[at + u, outs:rows, :] = scalar_rows(sq[u, 0:1, :])
+                out[at + u, 0:outs, :] = sums[:, u * BLOCK : (u + 1) * BLOCK].astype(kind)
+                if kind == F32:
+                    out[at + u, outs:rows, :] = jnp.broadcast_to(sq[u, 0:1, :], (EXTRA, BLOCK))
+                else:
+                    out[at + u, outs:rows, :] = scalar_rows(sq[u, 0:1, :])
             at = at + number
 
     operands = list(attended) + list(squares) + [weight, gains]
@@ -168,7 +160,7 @@
         body,
         in_specs=[IN_VMEM] * len(operands),
         out_specs=IN_VMEM,
-        out_shape=pltpu.VMEM((count, rows, BLOCK), BF16),
+        out_shape=pltpu.VMEM((count, rows, BLOCK), kind),
         name="project",
         compiler_params=ROOM,
     )(*in_vmem(*operands))
@@ -272,14 +264,45 @@
     )
 
 
-def ordered(own, other, axis, bit):
-    late = (lax.axis_index(axis) & bit) != 0
-    return jnp.where(late, jnp.concatenate([other, own]), jnp.concatenate([own, other]))
-
-
-def joined(pieces, low, high):
-    own, first, second, both = pieces
-    return ordered(ordered(own, first, "dp", low), ordered(second, both, "dp", low), "dp", high)
+def joined(pieces, bits):
+    size, columns, width = pieces[0].shape
+    place = lax.axis_index("dp").astype(jnp.int32).reshape(1)
+
+    def body(at, *refs):
+        out = refs[-1]
+        own = sum(jnp.where((at[0] & bit) != 0, 1 << n, 0) for n, bit in enumerate(bits))
+        for j, piece in enumerate(refs[:-1]):
+            out[pl.ds((own ^ j) * size, size)] = piece[...]
+
+    return pl.pallas_call(
+        body,
+        grid_spec=pltpu.PrefetchScalarGridSpec(
+            num_scalar_prefetch=1, grid=(1,), in_specs=[IN_VMEM] * len(pieces), out_specs=IN_VMEM
+        ),
+        out_shape=pltpu.VMEM((size * len(pieces), columns, width), BF16),
+        name="joined",
+        compiler_params=ROOM,
+    )(place, *in_vmem(*pieces))
+
+
+def gain_rows(norm_gain, width):
+    place = lax.axis_index("tensor").astype(jnp.int32).reshape(1)
+    count = width // BLOCK
+
+    def body(at, gain, out):
+        for n in range(count):
+            row = gain[pl.ds(at[0] * count + n, 1), :]
+            out[n * BLOCK : (n + 1) * BLOCK, :] = jnp.broadcast_to(row, (BLOCK, BLOCK)).T
+
+    return pl.pallas_call(
+        body,
+        grid_spec=pltpu.PrefetchScalarGridSpec(
+            num_scalar_prefetch=1, grid=(1,), in_specs=[IN_VMEM], out_specs=IN_VMEM
+        ),
+        out_shape=pltpu.VMEM((width, BLOCK), F32),
+        name="gain_rows",
+        compiler_params=ROOM,
+    )(place, norm_gain.reshape(-1, BLOCK))
 
 
 def on_device(query_rows, key_rows, value_rows, segment_ids, norm_gain, draft_weight, targets):
@@ -295,33 +318,34 @@
     segments = segment_ids.reshape(blocks, BLOCK)
     keys = lax.dynamic_slice_in_dim(key_rows, kv_head * HEAD_DIM, HEAD_DIM, 1)
     values = lax.dynamic_slice_in_dim(value_rows, kv_head * HEAD_DIM, HEAD_DIM, 1)
-    gain = lax.dynamic_slice_in_dim(norm_gain, place * width, width, 0)
-    gains = jnp.broadcast_to(gain[:, None], (width, BLOCK))
-
-    def attend(parity, first, count, *more):
+    gains = gain_rows(norm_gain, width)
+
+    def attend(parity, first, count):
         places = parity.astype(jnp.int32).reshape(1)
         return attention(
-            places, segment_ids, first, count, query_rows, keys, values, segments, *more
+            places, segment_ids, first, count, query_rows, keys, values, segments
         )
 
     half = blocks // 2
-    cuts = (0, half // 4, half - 3 * half // 8, half)
+    cut, last = half // 8, 3 * half // 4
     round_one = exchanges(draft_weight.T[None], 1, 2)
-    theirs_a = attend(1 - core, 0, cuts[1])
+    theirs_a = attend(1 - core, 0, cut)
     round_one, theirs_a = lax.optimization_barrier((round_one, theirs_a))
-    octet = joined(round_one, 1, 2)
-    round_two = exchange(octet, "dp", 4)
-    theirs_b = attend(1 - core, cuts[1], cuts[2] - cuts[1])
-    octet, round_two, theirs_b = lax.optimization_barrier((octet, round_two, theirs_b))
-    octet = ordered(octet, round_two, "dp", 4)
+    quarter = joined(round_one, (1, 2))
+    round_two = exchange(quarter, "dp", 4)
+    theirs_b = attend(1 - core, cut, half - cut)
+    quarter, round_two, theirs_b = lax.optimization_barrier((quarter, round_two, theirs_b))
+    octet = joined((quarter, round_two), (4,))
     round_three = exchange(octet, "dp", 8)
-    theirs_c = attend(1 - core, cuts[2], half - cuts[2])
-    octet, round_three, theirs_c = lax.optimization_barrier((octet, round_three, theirs_c))
-    weight = ordered(octet, round_three, "dp", 8).reshape(-1, width)
-
-    theirs, squares = zip(theirs_a, theirs_b, theirs_c)
-    received = exchange(project(theirs, squares, weight, gains), "tensor", 1)
-    mine, _, share = attend(core, 0, half, weight, gains)
+    mine_a = attend(core, 0, last)
+    octet, round_three, mine_a = lax.optimization_barrier((octet, round_three, mine_a))
+    weight = joined((octet, round_three), (8,)).reshape(-1, width)
+
+    theirs, squares = zip(theirs_a, theirs_b)
+    received = exchange(project(theirs, squares, weight, gains, BF16), "tensor", 1)
+    mine_b = attend(core, last, half - last)
+    mine, squares = zip(mine_a, mine_b)
+    share = project(mine, squares, weight, gains, F32)
     received, share = lax.optimization_barrier((received, share))
     parts = lax.all_to_all(
         together(share, received), "tensor", split_axis=0, concat_axis=0, tiled=True,
@@ -332,7 +356,7 @@
         copies, "tensor", split_axis=0, concat_axis=0, tiled=True, axis_index_groups=chips
     )
     their_slopes = exchange(my_slopes, "tensor", 1)
-    partial = gradient(my_slopes, (mine,), gains)
+    partial = gradient(my_slopes, mine, gains)
     partial = gradient(their_slopes, theirs, gains, partial)
     shares = partial.reshape(lax.axis_size("dp"), -1, width).astype(F16)
     shares = lax.all_to_all(shares, "dp", split_axis=0, concat_axis=0, tiled=True).astype(F32)

time: 117 us -> 104 us (0.89)
  other arithmetic: 5.55 us -> 0.88 us
  local copies, waits for them, and re-layouts: 5.48 us -> 1.94 us
  blocking collectives: 70.1 us -> 67.2 us
  Pallas kernels: 20.5 us -> 18.9 us
  waiting for transfers between devices: 3.73 us -> 2.23 us
    select_n x5 -> x0, other arithmetic: 4.67 us -> none  [ordered(): jnp.where(late, jnp.concatenate([other, own]), jnp.concatenate([own, othe...]
    unnamed x26 -> x10, local copies, waits for them, and re-layouts: 3.09 us -> 0.5 us
    pallas_call x4, Pallas kernels: 17.4 us -> 14.8 us  [attention(): pl.pallas_call(body, grid_spec=grid, out_shape=out_shape, name='attention...]
    all_to_all x1, blocking collectives: 23.9 us -> 21.9 us  [on_device(): lax.all_to_all(shares, 'dp', split_axis=0, concat_axis=0, tiled=True)]
    ppermute x7, waiting for transfers between devices: 3.73 us -> 2.23 us  [exchange(): return lax.ppermute(x, axis, [(i, i ^ bit) for i in range(size)])]
  transfers between devices with their start and end apart: 7 -> 7, of which waited for: 2 -> 2; matrix products, arithmetic and copies ran while one was open for 2% -> 1% of each run, Pallas kernels for 16% -> 16%
where the time goes in v3:
time: 104 us
  blocking collectives  67.2 us (65%)
  Pallas kernels  18.9 us (18%)
  starting transfers between devices  12.4 us (12%)
  waiting for transfers between devices  2.23 us (2%)
  local copies, waits for them, and re-layouts  1.94 us (2%)
    all_to_all x1, blocking collectives, on_device(): lax.all_to_all(together(share, received), 'tensor', split_axis=0, concat_...  25.2 us
    all_to_all x1, blocking collectives, on_device(): lax.all_to_all(shares, 'dp', split_axis=0, concat_axis=0, tiled=True)  21.9 us
    all_to_all x1, blocking collectives, on_device(): lax.all_to_all(copies, 'tensor', split_axis=0, concat_axis=0, tiled=True,...  20.1 us
    pallas_call x4, Pallas kernels, attention(): pl.pallas_call(body, grid_spec=grid, out_shape=out_shape, name='attention...  14.8 us
    ppermute x7, starting transfers between devices, exchange(): return lax.ppermute(x, axis, [(i, i ^ bit) for i in range(size)])  12.4 us
    ppermute x7, waiting for transfers between devices, exchange(): return lax.ppermute(x, axis, [(i, i ^ bit) for i in range(size)])  2.23 us
  transfers between devices with their start and end apart: 7, of which 2 were waited for; matrix products, arithmetic and copies ran while one was open for 1% of the time, Pallas kernels for 16%

profile of v3, /device:TPU:32, one launch (start us, length us, event | category | flops | bytes accessed | tf_op | source)
XLA Modules:
  0.0 103.7 jit_solution(10964517196272774573)
XLA Ops:
  0.0 1.9 %collective-permute-start.2 = (bf16[1,32,512]{2,1,0:T(8,128)(2,1)}, bf16[1,32,512]{2,1,0:T(8,128)(2,1)S(1)}, u32[]{:S(2)}, u32[]{:S(2)}) collective-permute-start(bf16[1,32,512]{2,1,0:T(8,128)(2,1)} %bitcast.20), channel_id=1, source_target_pairs={{0,48},{16,32},{32,16},{48,0},{64,112},{80,96},{96,80},{112,64},{1... | collective-permute-start | bytes 98312 | tf_op jit(solution)/shard_map/ppermute | solution.py:258
  1.9 2.3 %collective-permute-start.1 = (bf16[1,32,512]{2,1,0:T(8,128)(2,1)}, bf16[1,32,512]{2,1,0:T(8,128)(2,1)S(1)}, u32[]{:S(2)}, u32[]{:S(2)}) collective-permute-start(bf16[1,32,512]{2,1,0:T(8,128)(2,1)} %bitcast.21), channel_id=1, source_target_pairs={{0,32},{16,48},{32,0},{48,16},{64,96},{80,112},{96,64},{112,80},{1... | collective-permute-start | bytes 98312 | tf_op jit(solution)/shard_map/ppermute | solution.py:258
  4.2 0.6 collective-permute-start
  4.7 0.0 copy-start
  4.7 0.0 copy-start.1
  4.7 1.4 %constant_dynamic-slice_fusion = (bf16[2048,128]{1,0:T(8,128)(2,1)S(1)}, bf16[2048,128]{1,0:T(8,128)(2,1)S(1)}) fusion(bf16[2048,1024]{1,0:T(8,128)(2,1)} %param.9, s32[]{:T(128)S(6)} %select_n.17, bf16[2048,1024]{1,0:T(8,128)(2,1)} %param.8), kind=kLoop, calls=%fused_computation.3 | loop fusion | bytes 2097156 | tf_op jit(solution)/shard_map/dynamic_slice | solution.py:320
  6.2 0.5 copy-done
  6.7 0.0 copy-done.1
  6.7 0.0 copy-start.4
  6.7 1.3 %attention.4 = (bf16[1,512,128]{2,1,0:T(8,128)(2,1)S(1)}, f32[1,8,128]{2,1,0:T(8,128)S(1)}) custom-call(s32[1]{0:T(128)} %bitcast.3.place, s32[2048]{0:T(1024)S(1)} %copy-done.1, bf16[2048,512]{1,0:T(8,128)(2,1)S(1)} %copy-done, bf16[2048,128]{1,0:T(8,128)(2,1)S(1)} %get-tuple-element.54.refs_1_, bf16[2048,128]{1,0:T(8,128)(2,1)S(1)} %get-tuple-element.53.refs_2_, ...), custom_call_target="tpu_custom_call" | custom-call | tf_op jit(solution)/shard_map/attention/pallas_call | solution.py:128
  8.0 0.0 collective-permute-done.2.refs_3_
  8.0 0.0 collective-permute-done.1.refs_2_
  8.0 0.3 collective-permute-done.refs_1_
  8.3 0.0 copy-done.4
  8.3 5.6 %collective-permute-start.3 = (bf16[4,32,512]{2,1,0:T(8,128)(2,1)S(1)}, bf16[4,32,512]{2,1,0:T(8,128)(2,1)S(1)}, u32[]{:S(2)}, u32[]{:S(2)}) collective-permute-start(bf16[4,32,512]{2,1,0:T(8,128)(2,1)S(1)} %joined.3.refs_0_), channel_id=1, source_target_pairs={{0,64},{16,80},{32,96},{48,112},{64,0},{80,16},{96,32},{112,48},{1... | collective-permute-start | bytes 393224 | tf_op jit(solution)/shard_map/ppermute | solution.py:258
  13.9 6.0 %attention.5 = (bf16[7,512,128]{2,1,0:T(8,128)(2,1)S(1)}, f32[7,8,128]{2,1,0:T(8,128)S(1)}) custom-call(s32[1]{0:T(128)} %bitcast.3.place, s32[2048]{0:T(1024)S(1)} %copy-done.1, bf16[2048,512]{1,0:T(8,128)(2,1)S(1)} %copy-done, bf16[2048,128]{1,0:T(8,128)(2,1)S(1)} %get-tuple-element.54.refs_1_, bf16[2048,128]{1,0:T(8,128)(2,1)S(1)} %get-tuple-element.53.refs_2_, ...), custom_call_target="tpu_custom_call" | custom-call | tf_op jit(solution)/shard_map/attention/pallas_call | solution.py:128
  19.9 0.0 collective-permute-done.3.refs_1_
  19.9 1.8 %collective-permute-start.4 = (bf16[8,32,512]{2,1,0:T(8,128)(2,1)S(1)}, bf16[8,32,512]{2,1,0:T(8,128)(2,1)S(1)}, u32[]{:S(2)}, u32[]{:S(2)}) collective-permute-start(bf16[8,32,512]{2,1,0:T(8,128)(2,1)S(1)} %joined.4.refs_0_), channel_id=1, source_target_pairs={{0,128},{16,144},{32,160},{48,176},{64,192},{80,208},{96,224},{112... | collective-permute-start | bytes 786440 | tf_op jit(solution)/shard_map/ppermute | solution.py:258
  21.7 0.0 copy-start.3
  21.7 5.3 %attention.6 = (bf16[6,512,128]{2,1,0:T(8,128)(2,1)S(1)}, f32[6,8,128]{2,1,0:T(8,128)S(1)}) custom-call(s32[1]{0:T(128)} %bitcast.6.place, s32[2048]{0:T(1024)S(1)} %copy-done.1, bf16[2048,512]{1,0:T(8,128)(2,1)S(1)} %copy-done, bf16[2048,128]{1,0:T(8,128)(2,1)S(1)} %get-tuple-element.54.refs_1_, bf16[2048,128]{1,0:T(8,128)(2,1)S(1)} %get-tuple-element.53.refs_2_, ...), custom_call_target="tpu_custom_call" | custom-call | tf_op jit(solution)/shard_map/attention/pallas_call | solution.py:128
  27.0 0.0 copy-done.3
  27.0 0.1 gain_rows.1.refs_5_.refs_1_
  27.2 0.0 collective-permute-done.4.refs_1_
  27.2 0.9 project.2
  28.1 0.3 collective-permute-start.5
  28.4 2.2 %attention.7 = (bf16[2,512,128]{2,1,0:T(8,128)(2,1)S(1)}, f32[2,8,128]{2,1,0:T(8,128)S(1)}) custom-call(s32[1]{0:T(128)} %bitcast.6.place, s32[2048]{0:T(1024)S(1)} %copy-done.1, bf16[2048,512]{1,0:T(8,128)(2,1)S(1)} %copy-done, bf16[2048,128]{1,0:T(8,128)(2,1)S(1)} %get-tuple-element.54.refs_1_, bf16[2048,128]{1,0:T(8,128)(2,1)S(1)} %get-tuple-element.53.refs_2_, ...), custom_call_target="tpu_custom_call" | custom-call | tf_op jit(solution)/shard_map/attention/pallas_call | solution.py:128
  30.6 0.7 project.3.left
  31.4 0.0 collective-permute-done.5.right
  31.4 0.2 together.1
  31.6 0.0 copy-start.2
  31.6 25.2 %all_to_all.15.got = bf16[8,528,128]{2,1,0:T(8,128)(2,1)S(1)} all-to-all(bf16[8,528,128]{2,1,0:T(8,128)(2,1)S(1)} %together.1), channel_id=1, replica_groups={{0,2,4,6,8,10,12,14},{1,3,5,7,9,11,13,15},{16,18,20,22,24,26,28,30},{17..., dimensions={0} | all-to-all | bytes 2162688 | tf_op jit(solution)/shard_map/all_to_all | solution.py:350
  56.8 0.0 copy-done.2
  56.8 0.2 derive.1
  57.0 20.1 %all_to_all.16.refs_0_ = bf16[8,528,128]{2,1,0:T(8,128)(2,1)S(1)} all-to-all(bf16[8,528,128]{2,1,0:T(8,128)(2,1)S(1)} %derive.1), channel_id=1, replica_groups={{0,2,4,6,8,10,12,14},{1,3,5,7,9,11,13,15},{16,18,20,22,24,26,28,30},{17..., dimensions={0} | all-to-all | bytes 2162688 | tf_op jit(solution)/shard_map/all_to_all | solution.py:355
  77.1 0.0 collective-permute-start.6
  77.1 0.8 gradient.2.refs_4_
  77.9 1.9 %collective-permute-done.6.refs_0_ = bf16[8,528,128]{2,1,0:T(8,128)(2,1)S(1)} collective-permute-done((bf16[8,528,128]{2,1,0:T(8,128)(2,1)S(1)}, bf16[8,528,128]{2,1,0:T(8,128)(2,1)S(1)}, u32[]{:S(2)}, u32[]{:S(2)}) %collective-permute-start.6) | collective-permute-done | bytes 1081376 | tf_op jit(solution)/shard_map/ppermute | solution.py:258
  79.8 1.1 %gradient.3 = f32[512,512]{1,0:T(8,128)S(1)} custom-call(bf16[8,528,128]{2,1,0:T(8,128)(2,1)S(1)} %collective-permute-done.6.refs_0_, f32[512,128]{1,0:T(8,128)S(1)} %gain_rows.1.refs_5_.refs_1_, bf16[1,512,128]{2,1,0:T(8,128)(2,1)S(1)} %get-tuple-element.31.refs_0_.refs_2_, bf16[7,512,128]{2,1,0:T(8,128)(2,1)S(1)} %get-tuple-element.38.refs_1_.refs_3_, ...), custom_call_target="tpu_custom_call" | custom-call | tf_op jit(solution)/shard_map/gradient/pallas_call | solution.py:246
  80.9 0.1 convert_element_type.9
  81.0 21.9 %all_to_all.17 = f16[16,32,512]{2,1,0:T(8,128)(2,1)S(1)} all-to-all(f16[16,32,512]{2,1,0:T(8,128)(2,1)S(1)} %bitcast.24), channel_id=1, replica_groups=mesh['dp'=16,'tensor'=16] {'dp'}, dimensions={0} | all-to-all | bytes 1048576 | tf_op jit(solution)/shard_map/all_to_all | solution.py:362
  103.0 0.1 fusion
  103.1 0.6 multiply_bitcast_fusion
  (3 shorter events, 0.1 us)
Async XLA Ops:
  0.0 8.0 %collective-permute-start.2 = (bf16[1,32,512]{2,1,0:T(8,128)(2,1)}, bf16[1,32,512]{2,1,0:T(8,128)(2,1)S(1)}, u32[]{:S(2)}, u32[]{:S(2)}) collective-permute-start(bf16[1,32,512]{2,1,0:T(8,128)(2,1)} %bitcast.20), channel_id=1, source_target_pairs={{0,48},{16,32},{32,16},{48,0},{64,112},{80,96},{96,80},{112,64},{1... | collective-permute-start | bytes 98312 | tf_op jit(solution)/shard_map/ppermute | solution.py:258
  1.9 6.1 %collective-permute-start.1 = (bf16[1,32,512]{2,1,0:T(8,128)(2,1)}, bf16[1,32,512]{2,1,0:T(8,128)(2,1)S(1)}, u32[]{:S(2)}, u32[]{:S(2)}) collective-permute-start(bf16[1,32,512]{2,1,0:T(8,128)(2,1)} %bitcast.21), channel_id=1, source_target_pairs={{0,32},{16,48},{32,0},{48,16},{64,96},{80,112},{96,64},{112,80},{1... | collective-permute-start | bytes 98312 | tf_op jit(solution)/shard_map/ppermute | solution.py:258
  4.2 4.1 %collective-permute-start = (bf16[1,32,512]{2,1,0:T(8,128)(2,1)}, bf16[1,32,512]{2,1,0:T(8,128)(2,1)S(1)}, u32[]{:S(2)}, u32[]{:S(2)}) collective-permute-start(bf16[1,32,512]{2,1,0:T(8,128)(2,1)} %bitcast.22), channel_id=1, source_target_pairs={{0,16},{16,0},{32,48},{48,32},{64,80},{80,64},{96,112},{112,96},{1... | collective-permute-start | bytes 98312 | tf_op jit(solution)/shard_map/ppermute | solution.py:258
  4.7 1.9 %copy-start = (bf16[2048,512]{1,0:T(8,128)(2,1)S(1)}, bf16[2048,512]{1,0:T(8,128)(2,1)}, u32[]{:S(2)}) copy-start(bf16[2048,512]{1,0:T(8,128)(2,1)} %refs_0_.7) | copy-start | bytes 6291460
  4.7 1.9 %copy-start.1 = (s32[2048]{0:T(1024)S(1)}, s32[2048]{0:T(1024)}, u32[]{:S(2)}) copy-start(s32[2048]{0:T(1024)} %ids.7) | copy-start | bytes 24580
  6.7 1.6 %copy-start.4 = (bf16[512,32]{0,1:T(8,128)(2,1)S(1)}, bf16[512,32]{0,1:T(8,128)(2,1)}, u32[]{:S(2)}) copy-start(bf16[512,32]{0,1:T(8,128)(2,1)} %param.12) | copy-start | bytes 98308
  8.3 11.6 %collective-permute-start.3 = (bf16[4,32,512]{2,1,0:T(8,128)(2,1)S(1)}, bf16[4,32,512]{2,1,0:T(8,128)(2,1)S(1)}, u32[]{:S(2)}, u32[]{:S(2)}) collective-permute-start(bf16[4,32,512]{2,1,0:T(8,128)(2,1)S(1)} %joined.3.refs_0_), channel_id=1, source_target_pairs={{0,64},{16,80},{32,96},{48,112},{64,0},{80,16},{96,32},{112,48},{1... | collective-permute-start | bytes 393224 | tf_op jit(solution)/shard_map/ppermute | solution.py:258
  19.9 7.3 %collective-permute-start.4 = (bf16[8,32,512]{2,1,0:T(8,128)(2,1)S(1)}, bf16[8,32,512]{2,1,0:T(8,128)(2,1)S(1)}, u32[]{:S(2)}, u32[]{:S(2)}) collective-permute-start(bf16[8,32,512]{2,1,0:T(8,128)(2,1)S(1)} %joined.4.refs_0_), channel_id=1, source_target_pairs={{0,128},{16,144},{32,160},{48,176},{64,192},{80,208},{96,224},{112... | collective-permute-start | bytes 786440 | tf_op jit(solution)/shard_map/ppermute | solution.py:258
  21.7 5.3 %copy-start.3 = (f32[8192]{0:T(1024)S(1)}, f32[8192]{0:T(1024)}, u32[]{:S(2)}) copy-start(f32[8192]{0:T(1024)} %param.11) | copy-start | bytes 98308
  28.1 3.3 %collective-permute-start.5 = (bf16[8,528,128]{2,1,0:T(8,128)(2,1)S(1)}, bf16[8,528,128]{2,1,0:T(8,128)(2,1)S(1)}, u32[]{:S(2)}, u32[]{:S(2)}) collective-permute-start(bf16[8,528,128]{2,1,0:T(8,128)(2,1)S(1)} %project.2), channel_id=1, source_target_pairs={{0,1},{1,0},{2,3},{3,2},{4,5},{5,4},{6,7},{7,6},{8,9},{9,8},{10,11... | collective-permute-start | bytes 3244040 | tf_op jit(solution)/shard_map/ppermute | solution.py:258
  31.6 25.2 %copy-start.2 = (bf16[128,512]{1,0:T(8,128)(2,1)S(1)}, bf16[128,512]{1,0:T(8,128)(2,1)}, u32[]{:S(2)}) copy-start(bf16[128,512]{1,0:T(8,128)(2,1)} %want.1) | copy-start | bytes 393220
  77.1 2.7 %collective-permute-start.6 = (bf16[8,528,128]{2,1,0:T(8,128)(2,1)S(1)}, bf16[8,528,128]{2,1,0:T(8,128)(2,1)S(1)}, u32[]{:S(2)}, u32[]{:S(2)}) collective-permute-start(bf16[8,528,128]{2,1,0:T(8,128)(2,1)S(1)} %all_to_all.16.refs_0_), channel_id=1, source_target_pairs={{0,1},{1,0},{2,3},{3,2},{4,5},{5,4},{6,7},{7,6},{8,9},{9,8},{10,11... | collective-permute-start | bytes 3244040 | tf_op jit(solution)/shard_map/ppermute | solution.py:258

commit v4 on v3

--- a/solution.py
+++ b/solution.py
@@ -47,13 +47,14 @@
 ):
     length, width = query_rows.shape
     heads = width // HEAD_DIM
+    side = heads
     blocks = length // BLOCK
     most = min(blocks, DOC_MAX // BLOCK + 1)
     step = math.log2(math.e) * HEAD_DIM ** (-0.5)
 
     def body(place, ids, *refs):
         query, key, value, segment = refs[:4]
-        out, square = refs[-2:]
+        out = refs[-1]
         at = pl.program_id(0)
         block = (first + at) * 2 + place[0]
         needed = 1
@@ -84,24 +85,27 @@
             mine = segment[pl.ds(block, 1), :].astype(F32)
             same = jnp.concatenate(columns, axis=0) == mine
             bias = jnp.where(same & (key_at <= query_at), 0.0, -1e30)
-            stacked = jnp.concatenate(
-                [query[:, h * HEAD_DIM : (h + 1) * HEAD_DIM] for h in range(heads)], axis=0
-            )
-            scores = lax.dot_general(
-                key[pl.ds(start, window), :], stacked, (((1,), (1,)), ((), ())),
-                preferred_element_type=F32,
-            )
-            scores = scores + jnp.concatenate([bias] * heads, axis=1)
-            top = jnp.max(scores, axis=0, keepdims=True)
-            shifted = jnp.exp2((scores - top) * step)
-            inverse = 1.0 / jnp.sum(shifted, axis=0, keepdims=True)
-            probs = (shifted * inverse).astype(BF16)
-            mixed = lax.dot_general(
-                value[pl.ds(start, window), :], probs, (((0,), (0,)), ((), ())),
-                preferred_element_type=F32,
-            ).astype(BF16)
-            for h in range(heads):
-                out[at, h * HEAD_DIM : (h + 1) * HEAD_DIM, :] = mixed[:, h * BLOCK : (h + 1) * BLOCK]
+            bias = jnp.concatenate([bias] * side, axis=1)
+            near_keys, near_values = key[pl.ds(start, window), :], value[pl.ds(start, window), :]
+            for h in range(0, heads, side):
+                stacked = jnp.concatenate(
+                    [query[:, n * HEAD_DIM : (n + 1) * HEAD_DIM] for n in range(h, h + side)],
+                    axis=0,
+                )
+                scores = bias + lax.dot_general(
+                    near_keys, stacked, (((1,), (1,)), ((), ())), preferred_element_type=F32
+                )
+                top = jnp.max(scores, axis=0, keepdims=True)
+                shifted = jnp.exp2((scores - top) * step)
+                inverse = 1.0 / jnp.sum(shifted, axis=0, keepdims=True)
+                probs = (shifted * inverse).astype(BF16)
+                mixed = lax.dot_general(
+                    near_values, probs, (((0,), (0,)), ((), ())), preferred_element_type=F32
+                ).astype(BF16)
+                for n in range(side):
+                    out[at, (h + n) * HEAD_DIM : (h + n + 1) * HEAD_DIM, :] = mixed[
+                        :, n * BLOCK : (n + 1) * BLOCK
+                    ]
 
         below = 0
         for near in range(2, most + 1):
@@ -109,21 +113,14 @@
             pl.when(fits)(lambda near=near: over(near))
             below = near
 
-        wide = out[at].astype(F32)
-        total = jnp.sum(wide * wide, axis=0, keepdims=True)
-        square[at] = jnp.broadcast_to(total, (8, BLOCK))
-
     in_specs = [pl.BlockSpec((BLOCK, width), lambda i, s, d: ((first + i) * 2 + s[0], 0))]
-    out_shape = [
-        pltpu.VMEM((count, width, BLOCK), BF16),
-        pltpu.VMEM((count, 8, BLOCK), F32),
-    ]
+    out_shape = pltpu.VMEM((count, width, BLOCK), BF16)
     operands = [query_rows, *in_vmem(keys, values), segments]
     grid = pltpu.PrefetchScalarGridSpec(
         num_scalar_prefetch=2,
         grid=(count,),
         in_specs=in_specs + [IN_VMEM] * (len(operands) - 1),
-        out_specs=[IN_VMEM] * len(out_shape),
+        out_specs=IN_VMEM,
     )
     return pl.pallas_call(body, grid_spec=grid, out_shape=out_shape, name="attention",
         compiler_params=ROOM,
@@ -132,30 +129,30 @@
     )
 
 
-def project(attended, squares, weight, gains, kind):
+def project(attended, weight, gains, kind):
     outs = weight.shape[0]
     rows = outs + EXTRA
     pieces = len(attended)
     count = sum(x.shape[0] for x in attended)
 
     def body(*refs):
-        mat, gain, out = refs[2 * pieces], refs[2 * pieces + 1], refs[-1]
+        mat, gain, out = refs[pieces], refs[pieces + 1], refs[-1]
         at = 0
-        for att, sq in zip(refs[:pieces], refs[pieces : 2 * pieces]):
+        for att in refs[:pieces]:
             number = att.shape[0]
-            wide = jnp.concatenate(
-                [(att[u].astype(F32) * gain[...]).astype(BF16) for u in range(number)], axis=1
-            )
-            sums = jnp.dot(mat[...], wide, preferred_element_type=F32)
+            wide = [att[u].astype(F32) for u in range(number)]
+            scaled = jnp.concatenate([(x * gain[...]).astype(BF16) for x in wide], axis=1)
+            sums = jnp.dot(mat[...], scaled, preferred_element_type=F32)
             for u in range(number):
                 out[at + u, 0:outs, :] = sums[:, u * BLOCK : (u + 1) * BLOCK].astype(kind)
+                total = jnp.sum(wide[u] * wide[u], axis=0, keepdims=True)
                 if kind == F32:
-                    out[at + u, outs:rows, :] = jnp.broadcast_to(sq[u, 0:1, :], (EXTRA, BLOCK))
+                    out[at + u, outs:rows, :] = jnp.broadcast_to(total, (EXTRA, BLOCK))
                 else:
-                    out[at + u, outs:rows, :] = scalar_rows(sq[u, 0:1, :])
+                    out[at + u, outs:rows, :] = scalar_rows(total)
             at = at + number
 
-    operands = list(attended) + list(squares) + [weight, gains]
+    operands = list(attended) + [weight, gains]
     return pl.pallas_call(
         body,
         in_specs=[IN_VMEM] * len(operands),
@@ -341,11 +338,10 @@
     octet, round_three, mine_a = lax.optimization_barrier((octet, round_three, mine_a))
     weight = joined((octet, round_three), (8,)).reshape(-1, width)
 
-    theirs, squares = zip(theirs_a, theirs_b)
-    received = exchange(project(theirs, squares, weight, gains, BF16), "tensor", 1)
-    mine_b = attend(core, last, half - last)
-    mine, squares = zip(mine_a, mine_b)
-    share = project(mine, squares, weight, gains, F32)
+    theirs = (theirs_a, theirs_b)
+    received = exchange(project(theirs, weight, gains, BF16), "tensor", 1)
+    mine = (mine_a, attend(core, last, half - last))
+    share = project(mine, weight, gains, F32)
     received, share = lax.optimization_barrier((received, share))
     parts = lax.all_to_all(
         together(share, received), "tensor", split_axis=0, concat_axis=0, tiled=True,

time: 104 us -> 104 us (level)
  Pallas kernels: 18.9 us -> 17.8 us
    pallas_call x4, Pallas kernels: 14.8 us -> 13.7 us  [attention(): pl.pallas_call(body, grid_spec=grid, out_shape=out_shape, name='attention...]
  transfers between devices with their start and end apart: 7 -> 7, of which waited for: 2 -> 4; matrix products, arithmetic and copies ran while one was open for 1% -> 1% of each run, Pallas kernels for 16% -> 15%
where the time goes in v4:
time: 104 us; the launch traced here: 103 us
  blocking collectives  67.7 us (65%)
  Pallas kernels  17.8 us (17%)
  starting transfers between devices  11.9 us (11%)
  waiting for transfers between devices  3.12 us (3%)
  local copies, waits for them, and re-layouts  1.94 us (2%)
    all_to_all x1, blocking collectives, on_device(): lax.all_to_all(together(share, received), 'tensor', split_axis=0, concat_...  25.1 us
    all_to_all x1, blocking collectives, on_device(): lax.all_to_all(shares, 'dp', split_axis=0, concat_axis=0, tiled=True)  22.7 us
    all_to_all x1, blocking collectives, on_device(): lax.all_to_all(copies, 'tensor', split_axis=0, concat_axis=0, tiled=True,...  19.9 us
    pallas_call x4, Pallas kernels, attention(): pl.pallas_call(body, grid_spec=grid, out_shape=out_shape, name='attention...  13.7 us
    ppermute x7, starting transfers between devices, exchange(): return lax.ppermute(x, axis, [(i, i ^ bit) for i in range(size)])  11.9 us
    ppermute x7, waiting for transfers between devices, exchange(): return lax.ppermute(x, axis, [(i, i ^ bit) for i in range(size)])  3.12 us
  transfers between devices with their start and end apart: 7, of which 4 were waited for; matrix products, arithmetic and copies ran while one was open for 1% of the time, Pallas kernels for 15%

profile of v4, /device:TPU:32, one launch (start us, length us, event | category | flops | bytes accessed | tf_op | source)
XLA Modules:
  0.0 103.5 jit_solution(5271122023206448276)
XLA Ops:
  0.0 1.9 %collective-permute-start.2 = (bf16[1,32,512]{2,1,0:T(8,128)(2,1)}, bf16[1,32,512]{2,1,0:T(8,128)(2,1)S(1)}, u32[]{:S(2)}, u32[]{:S(2)}) collective-permute-start(bf16[1,32,512]{2,1,0:T(8,128)(2,1)} %bitcast.20), channel_id=1, source_target_pairs={{0,48},{16,32},{32,16},{48,0},{64,112},{80,96},{96,80},{112,64},{1... | collective-permute-start | bytes 98312 | tf_op jit(solution)/shard_map/ppermute | solution.py:255
  1.9 2.3 %collective-permute-start.1 = (bf16[1,32,512]{2,1,0:T(8,128)(2,1)}, bf16[1,32,512]{2,1,0:T(8,128)(2,1)S(1)}, u32[]{:S(2)}, u32[]{:S(2)}) collective-permute-start(bf16[1,32,512]{2,1,0:T(8,128)(2,1)} %bitcast.21), channel_id=1, source_target_pairs={{0,32},{16,48},{32,0},{48,16},{64,96},{80,112},{96,64},{112,80},{1... | collective-permute-start | bytes 98312 | tf_op jit(solution)/shard_map/ppermute | solution.py:255
  4.2 0.6 collective-permute-start
  4.7 0.0 copy-start
  4.7 0.0 copy-start.1
  4.7 1.4 %constant_dynamic-slice_fusion = (bf16[2048,128]{1,0:T(8,128)(2,1)S(1)}, bf16[2048,128]{1,0:T(8,128)(2,1)S(1)}) fusion(bf16[2048,1024]{1,0:T(8,128)(2,1)} %param.9, s32[]{:T(128)S(6)} %select_n.17, bf16[2048,1024]{1,0:T(8,128)(2,1)} %param.8), kind=kLoop, calls=%fused_computation.3 | loop fusion | bytes 2097156 | tf_op jit(solution)/shard_map/dynamic_slice | solution.py:317
  6.2 0.5 copy-done
  6.7 0.0 copy-done.1
  6.7 0.0 copy-start.4
  6.7 1.2 %attention.4.refs_0_.refs_2_ = bf16[1,512,128]{2,1,0:T(8,128)(2,1)S(1)} custom-call(s32[1]{0:T(128)} %bitcast.3.place, s32[2048]{0:T(1024)S(1)} %copy-done.1, bf16[2048,512]{1,0:T(8,128)(2,1)S(1)} %copy-done, bf16[2048,128]{1,0:T(8,128)(2,1)S(1)} %get-tuple-element.32.refs_1_, bf16[2048,128]{1,0:T(8,128)(2,1)S(1)} %get-tuple-element.31.refs_2_, ...), custom_call_target="tpu_custom_call" | custom-call | tf_op jit(solution)/shard_map/attention/pallas_call | solution.py:125
  7.9 0.0 collective-permute-done.2.refs_3_
  8.0 0.0 collective-permute-done.1.refs_2_
  8.0 0.3 collective-permute-done.refs_1_
  8.3 0.0 copy-done.4
  8.3 5.6 %collective-permute-start.3 = (bf16[4,32,512]{2,1,0:T(8,128)(2,1)S(1)}, bf16[4,32,512]{2,1,0:T(8,128)(2,1)S(1)}, u32[]{:S(2)}, u32[]{:S(2)}) collective-permute-start(bf16[4,32,512]{2,1,0:T(8,128)(2,1)S(1)} %joined.3.refs_0_), channel_id=1, source_target_pairs={{0,64},{16,80},{32,96},{48,112},{64,0},{80,16},{96,32},{112,48},{1... | collective-permute-start | bytes 393224 | tf_op jit(solution)/shard_map/ppermute | solution.py:255
  13.9 5.3 %attention.5.refs_1_.refs_3_ = bf16[7,512,128]{2,1,0:T(8,128)(2,1)S(1)} custom-call(s32[1]{0:T(128)} %bitcast.3.place, s32[2048]{0:T(1024)S(1)} %copy-done.1, bf16[2048,512]{1,0:T(8,128)(2,1)S(1)} %copy-done, bf16[2048,128]{1,0:T(8,128)(2,1)S(1)} %get-tuple-element.32.refs_1_, bf16[2048,128]{1,0:T(8,128)(2,1)S(1)} %get-tuple-element.31.refs_2_, ...), custom_call_target="tpu_custom_call" | custom-call | tf_op jit(solution)/shard_map/attention/pallas_call | solution.py:125
  19.2 0.1 collective-permute-done.3.refs_1_
  19.4 1.3 %collective-permute-start.4 = (bf16[8,32,512]{2,1,0:T(8,128)(2,1)S(1)}, bf16[8,32,512]{2,1,0:T(8,128)(2,1)S(1)}, u32[]{:S(2)}, u32[]{:S(2)}) collective-permute-start(bf16[8,32,512]{2,1,0:T(8,128)(2,1)S(1)} %joined.4.refs_0_), channel_id=1, source_target_pairs={{0,128},{16,144},{32,160},{48,176},{64,192},{80,208},{96,224},{112... | collective-permute-start | bytes 786440 | tf_op jit(solution)/shard_map/ppermute | solution.py:255
  20.7 0.0 copy-start.3
  20.7 4.8 %attention.6.refs_0_.refs_2_ = bf16[6,512,128]{2,1,0:T(8,128)(2,1)S(1)} custom-call(s32[1]{0:T(128)} %bitcast.6.place, s32[2048]{0:T(1024)S(1)} %copy-done.1, bf16[2048,512]{1,0:T(8,128)(2,1)S(1)} %copy-done, bf16[2048,128]{1,0:T(8,128)(2,1)S(1)} %get-tuple-element.32.refs_1_, bf16[2048,128]{1,0:T(8,128)(2,1)S(1)} %get-tuple-element.31.refs_2_, ...), custom_call_target="tpu_custom_call" | custom-call | tf_op jit(solution)/shard_map/attention/pallas_call | solution.py:125
  25.5 0.0 copy-done.3
  25.6 0.1 gain_rows.1.refs_3_.refs_1_
  25.7 0.7 collective-permute-done.4.refs_1_
  26.4 0.9 project.2
  27.3 0.3 collective-permute-start.5
  27.6 2.3 %attention.7.refs_1_.refs_3_ = bf16[2,512,128]{2,1,0:T(8,128)(2,1)S(1)} custom-call(s32[1]{0:T(128)} %bitcast.6.place, s32[2048]{0:T(1024)S(1)} %copy-done.1, bf16[2048,512]{1,0:T(8,128)(2,1)S(1)} %copy-done, bf16[2048,128]{1,0:T(8,128)(2,1)S(1)} %get-tuple-element.32.refs_1_, bf16[2048,128]{1,0:T(8,128)(2,1)S(1)} %get-tuple-element.31.refs_2_, ...), custom_call_target="tpu_custom_call" | custom-call | tf_op jit(solution)/shard_map/attention/pallas_call | solution.py:125
  29.9 0.8 project.3.left
  30.7 0.0 collective-permute-done.5.right
  30.7 0.2 together.1
  30.9 0.0 copy-start.2
  30.9 25.1 %all_to_all.15.got = bf16[8,528,128]{2,1,0:T(8,128)(2,1)S(1)} all-to-all(bf16[8,528,128]{2,1,0:T(8,128)(2,1)S(1)} %together.1), channel_id=1, replica_groups={{0,2,4,6,8,10,12,14},{1,3,5,7,9,11,13,15},{16,18,20,22,24,26,28,30},{17..., dimensions={0} | all-to-all | bytes 2162688 | tf_op jit(solution)/shard_map/all_to_all | solution.py:346
  56.0 0.0 copy-done.2
  56.0 0.2 derive.1
  56.2 19.9 %all_to_all.16.refs_0_ = bf16[8,528,128]{2,1,0:T(8,128)(2,1)S(1)} all-to-all(bf16[8,528,128]{2,1,0:T(8,128)(2,1)S(1)} %derive.1), channel_id=1, replica_groups={{0,2,4,6,8,10,12,14},{1,3,5,7,9,11,13,15},{16,18,20,22,24,26,28,30},{17..., dimensions={0} | all-to-all | bytes 2162688 | tf_op jit(solution)/shard_map/all_to_all | solution.py:351
  76.1 0.0 collective-permute-start.6
  76.1 0.8 gradient.2.refs_4_
  76.9 1.9 %collective-permute-done.6.refs_0_ = bf16[8,528,128]{2,1,0:T(8,128)(2,1)S(1)} collective-permute-done((bf16[8,528,128]{2,1,0:T(8,128)(2,1)S(1)}, bf16[8,528,128]{2,1,0:T(8,128)(2,1)S(1)}, u32[]{:S(2)}, u32[]{:S(2)}) %collective-permute-start.6) | collective-permute-done | bytes 1081376 | tf_op jit(solution)/shard_map/ppermute | solution.py:255
  78.8 1.1 %gradient.3 = f32[512,512]{1,0:T(8,128)S(1)} custom-call(bf16[8,528,128]{2,1,0:T(8,128)(2,1)S(1)} %collective-permute-done.6.refs_0_, f32[512,128]{1,0:T(8,128)S(1)} %gain_rows.1.refs_3_.refs_1_, bf16[1,512,128]{2,1,0:T(8,128)(2,1)S(1)} %attention.4.refs_0_.refs_2_, bf16[7,512,128]{2,1,0:T(8,128)(2,1)S(1)} %attention.5.refs_1_.refs_3_, ...), custom_call_target="tpu_custom_call" | custom-call | tf_op jit(solution)/shard_map/gradient/pallas_call | solution.py:243
  79.9 0.1 convert_element_type.9
  80.0 22.7 %all_to_all.17 = f16[16,32,512]{2,1,0:T(8,128)(2,1)S(1)} all-to-all(f16[16,32,512]{2,1,0:T(8,128)(2,1)S(1)} %bitcast.24), channel_id=1, replica_groups=mesh['dp'=16,'tensor'=16] {'dp'}, dimensions={0} | all-to-all | bytes 1048576 | tf_op jit(solution)/shard_map/all_to_all | solution.py:358
  102.7 0.1 fusion
  102.8 0.6 multiply_bitcast_fusion
  (3 shorter events, 0.1 us)
Async XLA Ops:
  0.0 7.9 %collective-permute-start.2 = (bf16[1,32,512]{2,1,0:T(8,128)(2,1)}, bf16[1,32,512]{2,1,0:T(8,128)(2,1)S(1)}, u32[]{:S(2)}, u32[]{:S(2)}) collective-permute-start(bf16[1,32,512]{2,1,0:T(8,128)(2,1)} %bitcast.20), channel_id=1, source_target_pairs={{0,48},{16,32},{32,16},{48,0},{64,112},{80,96},{96,80},{112,64},{1... | collective-permute-start | bytes 98312 | tf_op jit(solution)/shard_map/ppermute | solution.py:255
  1.9 6.0 %collective-permute-start.1 = (bf16[1,32,512]{2,1,0:T(8,128)(2,1)}, bf16[1,32,512]{2,1,0:T(8,128)(2,1)S(1)}, u32[]{:S(2)}, u32[]{:S(2)}) collective-permute-start(bf16[1,32,512]{2,1,0:T(8,128)(2,1)} %bitcast.21), channel_id=1, source_target_pairs={{0,32},{16,48},{32,0},{48,16},{64,96},{80,112},{96,64},{112,80},{1... | collective-permute-start | bytes 98312 | tf_op jit(solution)/shard_map/ppermute | solution.py:255
  4.2 4.1 %collective-permute-start = (bf16[1,32,512]{2,1,0:T(8,128)(2,1)}, bf16[1,32,512]{2,1,0:T(8,128)(2,1)S(1)}, u32[]{:S(2)}, u32[]{:S(2)}) collective-permute-start(bf16[1,32,512]{2,1,0:T(8,128)(2,1)} %bitcast.22), channel_id=1, source_target_pairs={{0,16},{16,0},{32,48},{48,32},{64,80},{80,64},{96,112},{112,96},{1... | collective-permute-start | bytes 98312 | tf_op jit(solution)/shard_map/ppermute | solution.py:255
  4.7 1.9 %copy-start = (bf16[2048,512]{1,0:T(8,128)(2,1)S(1)}, bf16[2048,512]{1,0:T(8,128)(2,1)}, u32[]{:S(2)}) copy-start(bf16[2048,512]{1,0:T(8,128)(2,1)} %refs_0_.7) | copy-start | bytes 6291460
  4.7 1.9 %copy-start.1 = (s32[2048]{0:T(1024)S(1)}, s32[2048]{0:T(1024)}, u32[]{:S(2)}) copy-start(s32[2048]{0:T(1024)} %ids.7) | copy-start | bytes 24580
  6.7 1.6 %copy-start.4 = (bf16[512,32]{0,1:T(8,128)(2,1)S(1)}, bf16[512,32]{0,1:T(8,128)(2,1)}, u32[]{:S(2)}) copy-start(bf16[512,32]{0,1:T(8,128)(2,1)} %param.12) | copy-start | bytes 98308
  8.3 11.0 %collective-permute-start.3 = (bf16[4,32,512]{2,1,0:T(8,128)(2,1)S(1)}, bf16[4,32,512]{2,1,0:T(8,128)(2,1)S(1)}, u32[]{:S(2)}, u32[]{:S(2)}) collective-permute-start(bf16[4,32,512]{2,1,0:T(8,128)(2,1)S(1)} %joined.3.refs_0_), channel_id=1, source_target_pairs={{0,64},{16,80},{32,96},{48,112},{64,0},{80,16},{96,32},{112,48},{1... | collective-permute-start | bytes 393224 | tf_op jit(solution)/shard_map/ppermute | solution.py:255
  19.4 7.0 %collective-permute-start.4 = (bf16[8,32,512]{2,1,0:T(8,128)(2,1)S(1)}, bf16[8,32,512]{2,1,0:T(8,128)(2,1)S(1)}, u32[]{:S(2)}, u32[]{:S(2)}) collective-permute-start(bf16[8,32,512]{2,1,0:T(8,128)(2,1)S(1)} %joined.4.refs_0_), channel_id=1, source_target_pairs={{0,128},{16,144},{32,160},{48,176},{64,192},{80,208},{96,224},{112... | collective-permute-start | bytes 786440 | tf_op jit(solution)/shard_map/ppermute | solution.py:255
  20.7 4.8 %copy-start.3 = (f32[8192]{0:T(1024)S(1)}, f32[8192]{0:T(1024)}, u32[]{:S(2)}) copy-start(f32[8192]{0:T(1024)} %param.11) | copy-start | bytes 98308
  27.3 3.4 %collective-permute-start.5 = (bf16[8,528,128]{2,1,0:T(8,128)(2,1)S(1)}, bf16[8,528,128]{2,1,0:T(8,128)(2,1)S(1)}, u32[]{:S(2)}, u32[]{:S(2)}) collective-permute-start(bf16[8,528,128]{2,1,0:T(8,128)(2,1)S(1)} %project.2), channel_id=1, source_target_pairs={{0,1},{1,0},{2,3},{3,2},{4,5},{5,4},{6,7},{7,6},{8,9},{9,8},{10,11... | collective-permute-start | bytes 3244040 | tf_op jit(solution)/shard_map/ppermute | solution.py:255
  30.9 25.1 %copy-start.2 = (bf16[128,512]{1,0:T(8,128)(2,1)S(1)}, bf16[128,512]{1,0:T(8,128)(2,1)}, u32[]{:S(2)}) copy-start(bf16[128,512]{1,0:T(8,128)(2,1)} %want.1) | copy-start | bytes 393220
  76.1 2.7 %collective-permute-start.6 = (bf16[8,528,128]{2,1,0:T(8,128)(2,1)S(1)}, bf16[8,528,128]{2,1,0:T(8,128)(2,1)S(1)}, u32[]{:S(2)}, u32[]{:S(2)}) collective-permute-start(bf16[8,528,128]{2,1,0:T(8,128)(2,1)S(1)} %all_to_all.16.refs_0_), channel_id=1, source_target_pairs={{0,1},{1,0},{2,3},{3,2},{4,5},{5,4},{6,7},{7,6},{8,9},{9,8},{10,11... | collective-permute-start | bytes 3244040 | tf_op jit(solution)/shard_map/ppermute | solution.py:255

commit v5 on v4

--- a/solution.py
+++ b/solution.py
@@ -16,6 +16,7 @@
 BF16 = jnp.bfloat16
 F32 = jnp.float32
 F16 = jnp.float16
+RING = 8
 ROOT_SCALE = 2.0**20
 
 
@@ -255,28 +256,29 @@
     return lax.ppermute(x, axis, [(i, i ^ bit) for i in range(size)])
 
 
-def exchanges(x, low, high):
-    return (
-        x, exchange(x, "dp", low), exchange(x, "dp", high), exchange(x, "dp", low | high)
-    )
-
-
-def joined(pieces, bits):
-    size, columns, width = pieces[0].shape
+def shifted(x, step):
+    size = lax.axis_size("dp")
+    return lax.ppermute(
+        x, "dp", [(i, i - i % RING + (i - step) % RING) for i in range(size)]
+    )
+
+
+def joined(pieces, slots, count):
+    _, columns, width = pieces[0].shape
     place = lax.axis_index("dp").astype(jnp.int32).reshape(1)
 
     def body(at, *refs):
         out = refs[-1]
-        own = sum(jnp.where((at[0] & bit) != 0, 1 << n, 0) for n, bit in enumerate(bits))
         for j, piece in enumerate(refs[:-1]):
-            out[pl.ds((own ^ j) * size, size)] = piece[...]
+            for n, slot in enumerate(slots(at[0], j)):
+                out[slot] = piece[n]
 
     return pl.pallas_call(
         body,
         grid_spec=pltpu.PrefetchScalarGridSpec(
             num_scalar_prefetch=1, grid=(1,), in_specs=[IN_VMEM] * len(pieces), out_specs=IN_VMEM
         ),
-        out_shape=pltpu.VMEM((size * len(pieces), columns, width), BF16),
+        out_shape=pltpu.VMEM((count, columns, width), BF16),
         name="joined",
         compiler_params=ROOM,
     )(place, *in_vmem(*pieces))
@@ -325,18 +327,31 @@
 
     half = blocks // 2
     cut, last = half // 8, 3 * half // 4
-    round_one = exchanges(draft_weight.T[None], 1, 2)
+    shard = draft_weight.T[None]
+    ahead, behind = shifted(shard, 1), shifted(shard, -1)
     theirs_a = attend(1 - core, 0, cut)
-    round_one, theirs_a = lax.optimization_barrier((round_one, theirs_a))
-    quarter = joined(round_one, (1, 2))
-    round_two = exchange(quarter, "dp", 4)
+    ahead, behind, theirs_a = lax.optimization_barrier((ahead, behind, theirs_a))
+    trio = joined((behind, shard, ahead), lambda place, j: (j,), 3)
+    duo = joined((shard, ahead), lambda place, j: (j,), 2)
+    far_ahead, far_behind = shifted(trio, 3), shifted(duo, -3)
     theirs_b = attend(1 - core, cut, half - cut)
-    quarter, round_two, theirs_b = lax.optimization_barrier((quarter, round_two, theirs_b))
-    octet = joined((quarter, round_two), (4,))
-    round_three = exchange(octet, "dp", 8)
+    trio, far_ahead, far_behind, theirs_b = lax.optimization_barrier(
+        (trio, far_ahead, far_behind, theirs_b)
+    )
+    starts = (RING - 1, 2, RING - 3)
+    octet = joined(
+        (trio, far_ahead, far_behind),
+        lambda place, j: [(place + starts[j] + n) % RING for n in range(3 if j < 2 else 2)],
+        RING,
+    )
+    other = exchange(octet, "dp", RING)
     mine_a = attend(core, 0, last)
-    octet, round_three, mine_a = lax.optimization_barrier((octet, round_three, mine_a))
-    weight = joined((octet, round_three), (8,)).reshape(-1, width)
+    octet, other, mine_a = lax.optimization_barrier((octet, other, mine_a))
+    weight = joined(
+        (octet, other),
+        lambda place, j: [(place // RING ^ j) * RING + n for n in range(RING)],
+        2 * RING,
+    ).reshape(-1, width)
 
     theirs = (theirs_a, theirs_b)
     received = exchange(project(theirs, weight, gains, BF16), "tensor", 1)

time: 104 us -> 102 us (0.981)
  blocking collectives: 67.7 us -> 66 us
  waiting for transfers between devices: 3.12 us -> 4.78 us
  starting transfers between devices: 11.9 us -> 10.3 us
    ppermute x7 -> x3, starting transfers between devices: 11.9 us -> 1.85 us  [exchange(): return lax.ppermute(x, axis, [(i, i ^ bit) for i in range(size)])]
    ppermute x0 -> x4, starting transfers between devices: none -> 8.47 us  [shifted(): lax.ppermute(x, 'dp', [(i, i - i % RING + (i - step) % RING) for i in ran...]
    ppermute x0 -> x4, waiting for transfers between devices: none -> 2.85 us  [shifted(): lax.ppermute(x, 'dp', [(i, i - i % RING + (i - step) % RING) for i in ran...]
    all_to_all x1, blocking collectives: 22.7 us -> 21.2 us  [on_device(): lax.all_to_all(shares, 'dp', split_axis=0, concat_axis=0, tiled=True)]
    ppermute x7 -> x3, waiting for transfers between devices: 3.12 us -> 1.94 us  [exchange(): return lax.ppermute(x, axis, [(i, i ^ bit) for i in range(size)])]
  transfers between devices with their start and end apart: 7 -> 7, of which waited for: 4 -> 3; matrix products, arithmetic and copies ran while one was open for 1% -> 1% of each run, Pallas kernels for 15% -> 15%
where the time goes in v5:
time: 102 us
  blocking collectives  66 us (65%)
  Pallas kernels  18 us (18%)
  starting transfers between devices  10.3 us (10%)
  waiting for transfers between devices  4.78 us (5%)
  local copies, waits for them, and re-layouts  1.94 us (2%)
    all_to_all x1, blocking collectives, on_device(): lax.all_to_all(together(share, received), 'tensor', split_axis=0, concat_...  24.9 us
    all_to_all x1, blocking collectives, on_device(): lax.all_to_all(shares, 'dp', split_axis=0, concat_axis=0, tiled=True)  21.2 us
    all_to_all x1, blocking collectives, on_device(): lax.all_to_all(copies, 'tensor', split_axis=0, concat_axis=0, tiled=True,...  19.9 us
    pallas_call x4, Pallas kernels, attention(): pl.pallas_call(body, grid_spec=grid, out_shape=out_shape, name='attention...  13.8 us
    ppermute x4, starting transfers between devices, shifted(): lax.ppermute(x, 'dp', [(i, i - i % RING + (i - step) % RING) for i in ran...  8.47 us
    ppermute x4, waiting for transfers between devices, shifted(): lax.ppermute(x, 'dp', [(i, i - i % RING + (i - step) % RING) for i in ran...  2.85 us
  transfers between devices with their start and end apart: 7, of which 3 were waited for; matrix products, arithmetic and copies ran while one was open for 1% of the time, Pallas kernels for 15%

profile of v5, /device:TPU:32, one launch (start us, length us, event | category | flops | bytes accessed | tf_op | source)
XLA Modules:
  0.0 102.1 jit_solution(17626832958037704715)
XLA Ops:
  0.0 1.9 %collective-permute-start.1 = (bf16[1,32,512]{2,1,0:T(8,128)(2,1)}, bf16[1,32,512]{2,1,0:T(8,128)(2,1)S(1)}, u32[]{:S(2)}, u32[]{:S(2)}) collective-permute-start(bf16[1,32,512]{2,1,0:T(8,128)(2,1)} %bitcast.19), channel_id=1, source_target_pairs={{0,16},{16,32},{32,48},{48,64},{64,80},{80,96},{96,112},{112,0},{1... | collective-permute-start | bytes 98312 | tf_op jit(solution)/shard_map/ppermute | solution.py:261
  1.9 0.1 collective-permute-start
  2.0 0.0 copy-start
  2.0 0.0 copy-start.1
  2.0 1.4 %constant_dynamic-slice_fusion = (bf16[2048,128]{1,0:T(8,128)(2,1)S(1)}, bf16[2048,128]{1,0:T(8,128)(2,1)S(1)}) fusion(bf16[2048,1024]{1,0:T(8,128)(2,1)} %param.9, s32[]{:T(128)S(6)} %select_n.17, bf16[2048,1024]{1,0:T(8,128)(2,1)} %param.8), kind=kLoop, calls=%fused_computation.3 | loop fusion | bytes 2097156 | tf_op jit(solution)/shard_map/dynamic_slice | solution.py:319
  3.5 0.5 copy-done
  4.0 0.0 copy-done.1
  4.0 0.0 copy-start.3
  4.0 1.2 %attention.4.refs_0_.refs_2_ = bf16[1,512,128]{2,1,0:T(8,128)(2,1)S(1)} custom-call(s32[1]{0:T(128)} %bitcast.3.place, s32[2048]{0:T(1024)S(1)} %copy-done.1, bf16[2048,512]{1,0:T(8,128)(2,1)S(1)} %copy-done, bf16[2048,128]{1,0:T(8,128)(2,1)S(1)} %get-tuple-element.30.refs_1_, bf16[2048,128]{1,0:T(8,128)(2,1)S(1)} %get-tuple-element.29.refs_2_, ...), custom_call_target="tpu_custom_call" | custom-call | tf_op jit(solution)/shard_map/attention/pallas_call | solution.py:126
  5.2 0.0 collective-permute-done.1.refs_0_
  5.2 0.8 collective-permute-done.refs_2_.refs_1_
  6.0 0.0 copy-done.3
  6.1 5.1 %collective-permute-start.2 = (bf16[3,32,512]{2,1,0:T(8,128)(2,1)S(1)}, bf16[3,32,512]{2,1,0:T(8,128)(2,1)S(1)}, u32[]{:S(2)}, u32[]{:S(2)}) collective-permute-start(bf16[3,32,512]{2,1,0:T(8,128)(2,1)S(1)} %joined.4.refs_0_), channel_id=1, source_target_pairs={{0,80},{16,96},{32,112},{48,0},{64,16},{80,32},{96,48},{112,64},{1... | collective-permute-start | bytes 294920 | tf_op jit(solution)/shard_map/ppermute | solution.py:261
  11.2 1.3 %collective-permute-start.3 = (bf16[2,32,512]{2,1,0:T(8,128)(2,1)S(1)}, bf16[2,32,512]{2,1,0:T(8,128)(2,1)S(1)}, u32[]{:S(2)}, u32[]{:S(2)}) collective-permute-start(bf16[2,32,512]{2,1,0:T(8,128)(2,1)S(1)} %joined.5), channel_id=1, source_target_pairs={{0,48},{16,64},{32,80},{48,96},{64,112},{80,0},{96,16},{112,32},{1... | collective-permute-start | bytes 196616 | tf_op jit(solution)/shard_map/ppermute | solution.py:261
  12.5 5.4 %attention.5.refs_1_.refs_3_ = bf16[7,512,128]{2,1,0:T(8,128)(2,1)S(1)} custom-call(s32[1]{0:T(128)} %bitcast.3.place, s32[2048]{0:T(1024)S(1)} %copy-done.1, bf16[2048,512]{1,0:T(8,128)(2,1)S(1)} %copy-done, bf16[2048,128]{1,0:T(8,128)(2,1)S(1)} %get-tuple-element.30.refs_1_, bf16[2048,128]{1,0:T(8,128)(2,1)S(1)} %get-tuple-element.29.refs_2_, ...), custom_call_target="tpu_custom_call" | custom-call | tf_op jit(solution)/shard_map/attention/pallas_call | solution.py:126
  17.9 2.0 %collective-permute-done.3.refs_2_ = bf16[2,32,512]{2,1,0:T(8,128)(2,1)S(1)} collective-permute-done((bf16[2,32,512]{2,1,0:T(8,128)(2,1)S(1)}, bf16[2,32,512]{2,1,0:T(8,128)(2,1)S(1)}, u32[]{:S(2)}, u32[]{:S(2)}) %collective-permute-start.3) | collective-permute-done | bytes 65568 | tf_op jit(solution)/shard_map/ppermute | solution.py:261
  20.0 0.0 collective-permute-done.2.refs_1_
  20.0 1.6 %collective-permute-start.4 = (bf16[8,32,512]{2,1,0:T(8,128)(2,1)S(1)}, bf16[8,32,512]{2,1,0:T(8,128)(2,1)S(1)}, u32[]{:S(2)}, u32[]{:S(2)}) collective-permute-start(bf16[8,32,512]{2,1,0:T(8,128)(2,1)S(1)} %joined.6.refs_0_), channel_id=1, source_target_pairs={{0,128},{16,144},{32,160},{48,176},{64,192},{80,208},{96,224},{112... | collective-permute-start | bytes 786440 | tf_op jit(solution)/shard_map/ppermute | solution.py:256
  21.6 0.0 copy-start.4
  21.6 4.9 %attention.6.refs_0_.refs_2_ = bf16[6,512,128]{2,1,0:T(8,128)(2,1)S(1)} custom-call(s32[1]{0:T(128)} %bitcast.6.place, s32[2048]{0:T(1024)S(1)} %copy-done.1, bf16[2048,512]{1,0:T(8,128)(2,1)S(1)} %copy-done, bf16[2048,128]{1,0:T(8,128)(2,1)S(1)} %get-tuple-element.30.refs_1_, bf16[2048,128]{1,0:T(8,128)(2,1)S(1)} %get-tuple-element.29.refs_2_, ...), custom_call_target="tpu_custom_call" | custom-call | tf_op jit(solution)/shard_map/attention/pallas_call | solution.py:126
  26.5 0.0 copy-done.4
  26.6 0.1 gain_rows.1.refs_3_.refs_1_
  26.7 0.0 collective-permute-done.4.refs_1_
  26.8 0.9 project.2
  27.6 0.3 collective-permute-start.5
  27.9 2.2 %attention.7.refs_1_.refs_3_ = bf16[2,512,128]{2,1,0:T(8,128)(2,1)S(1)} custom-call(s32[1]{0:T(128)} %bitcast.6.place, s32[2048]{0:T(1024)S(1)} %copy-done.1, bf16[2048,512]{1,0:T(8,128)(2,1)S(1)} %copy-done, bf16[2048,128]{1,0:T(8,128)(2,1)S(1)} %get-tuple-element.30.refs_1_, bf16[2048,128]{1,0:T(8,128)(2,1)S(1)} %get-tuple-element.29.refs_2_, ...), custom_call_target="tpu_custom_call" | custom-call | tf_op jit(solution)/shard_map/attention/pallas_call | solution.py:126
  30.1 0.8 project.3.left
  30.9 0.0 collective-permute-done.5.right
  30.9 0.2 together.1
  31.1 0.0 copy-start.2
  31.2 24.9 %all_to_all.15.got = bf16[8,528,128]{2,1,0:T(8,128)(2,1)S(1)} all-to-all(bf16[8,528,128]{2,1,0:T(8,128)(2,1)S(1)} %together.1), channel_id=1, replica_groups={{0,2,4,6,8,10,12,14},{1,3,5,7,9,11,13,15},{16,18,20,22,24,26,28,30},{17..., dimensions={0} | all-to-all | bytes 2162688 | tf_op jit(solution)/shard_map/all_to_all | solution.py:361
  56.1 0.0 copy-done.2
  56.1 0.2 derive.1
  56.3 19.9 %all_to_all.16.refs_0_ = bf16[8,528,128]{2,1,0:T(8,128)(2,1)S(1)} all-to-all(bf16[8,528,128]{2,1,0:T(8,128)(2,1)S(1)} %derive.1), channel_id=1, replica_groups={{0,2,4,6,8,10,12,14},{1,3,5,7,9,11,13,15},{16,18,20,22,24,26,28,30},{17..., dimensions={0} | all-to-all | bytes 2162688 | tf_op jit(solution)/shard_map/all_to_all | solution.py:366
  76.2 0.0 collective-permute-start.6
  76.2 0.8 gradient.2.refs_4_
  77.0 1.9 %collective-permute-done.6.refs_0_ = bf16[8,528,128]{2,1,0:T(8,128)(2,1)S(1)} collective-permute-done((bf16[8,528,128]{2,1,0:T(8,128)(2,1)S(1)}, bf16[8,528,128]{2,1,0:T(8,128)(2,1)S(1)}, u32[]{:S(2)}, u32[]{:S(2)}) %collective-permute-start.6) | collective-permute-done | bytes 1081376 | tf_op jit(solution)/shard_map/ppermute | solution.py:256
  79.0 1.1 %gradient.3 = f32[512,512]{1,0:T(8,128)S(1)} custom-call(bf16[8,528,128]{2,1,0:T(8,128)(2,1)S(1)} %collective-permute-done.6.refs_0_, f32[512,128]{1,0:T(8,128)S(1)} %gain_rows.1.refs_3_.refs_1_, bf16[1,512,128]{2,1,0:T(8,128)(2,1)S(1)} %attention.4.refs_0_.refs_2_, bf16[7,512,128]{2,1,0:T(8,128)(2,1)S(1)} %attention.5.refs_1_.refs_3_, ...), custom_call_target="tpu_custom_call" | custom-call | tf_op jit(solution)/shard_map/gradient/pallas_call | solution.py:244
  80.0 0.1 convert_element_type.9
  80.1 21.2 %all_to_all.17 = f16[16,32,512]{2,1,0:T(8,128)(2,1)S(1)} all-to-all(f16[16,32,512]{2,1,0:T(8,128)(2,1)S(1)} %bitcast.24), channel_id=1, replica_groups=mesh['dp'=16,'tensor'=16] {'dp'}, dimensions={0} | all-to-all | bytes 1048576 | tf_op jit(solution)/shard_map/all_to_all | solution.py:373
  101.3 0.1 fusion
  101.4 0.6 multiply_bitcast_fusion
  (4 shorter events, 0.1 us)
Async XLA Ops:
  0.0 5.2 %collective-permute-start.1 = (bf16[1,32,512]{2,1,0:T(8,128)(2,1)}, bf16[1,32,512]{2,1,0:T(8,128)(2,1)S(1)}, u32[]{:S(2)}, u32[]{:S(2)}) collective-permute-start(bf16[1,32,512]{2,1,0:T(8,128)(2,1)} %bitcast.19), channel_id=1, source_target_pairs={{0,16},{16,32},{32,48},{48,64},{64,80},{80,96},{96,112},{112,0},{1... | collective-permute-start | bytes 98312 | tf_op jit(solution)/shard_map/ppermute | solution.py:261
  1.9 4.1 %collective-permute-start = (bf16[1,32,512]{2,1,0:T(8,128)(2,1)}, bf16[1,32,512]{2,1,0:T(8,128)(2,1)S(1)}, u32[]{:S(2)}, u32[]{:S(2)}) collective-permute-start(bf16[1,32,512]{2,1,0:T(8,128)(2,1)} %bitcast.20), channel_id=1, source_target_pairs={{0,112},{16,0},{32,16},{48,32},{64,48},{80,64},{96,80},{112,96},{1... | collective-permute-start | bytes 98312 | tf_op jit(solution)/shard_map/ppermute | solution.py:261
  2.0 1.9 %copy-start = (bf16[2048,512]{1,0:T(8,128)(2,1)S(1)}, bf16[2048,512]{1,0:T(8,128)(2,1)}, u32[]{:S(2)}) copy-start(bf16[2048,512]{1,0:T(8,128)(2,1)} %refs_0_.7) | copy-start | bytes 6291460
  2.0 1.9 %copy-start.1 = (s32[2048]{0:T(1024)S(1)}, s32[2048]{0:T(1024)}, u32[]{:S(2)}) copy-start(s32[2048]{0:T(1024)} %ids.7) | copy-start | bytes 24580
  4.0 2.1 %copy-start.3 = (bf16[512,32]{0,1:T(8,128)(2,1)S(1)}, bf16[512,32]{0,1:T(8,128)(2,1)}, u32[]{:S(2)}) copy-start(bf16[512,32]{0,1:T(8,128)(2,1)} %param.12) | copy-start | bytes 98308
  6.1 13.9 %collective-permute-start.2 = (bf16[3,32,512]{2,1,0:T(8,128)(2,1)S(1)}, bf16[3,32,512]{2,1,0:T(8,128)(2,1)S(1)}, u32[]{:S(2)}, u32[]{:S(2)}) collective-permute-start(bf16[3,32,512]{2,1,0:T(8,128)(2,1)S(1)} %joined.4.refs_0_), channel_id=1, source_target_pairs={{0,80},{16,96},{32,112},{48,0},{64,16},{80,32},{96,48},{112,64},{1... | collective-permute-start | bytes 294920 | tf_op jit(solution)/shard_map/ppermute | solution.py:261
  11.2 8.8 %collective-permute-start.3 = (bf16[2,32,512]{2,1,0:T(8,128)(2,1)S(1)}, bf16[2,32,512]{2,1,0:T(8,128)(2,1)S(1)}, u32[]{:S(2)}, u32[]{:S(2)}) collective-permute-start(bf16[2,32,512]{2,1,0:T(8,128)(2,1)S(1)} %joined.5), channel_id=1, source_target_pairs={{0,48},{16,64},{32,80},{48,96},{64,112},{80,0},{96,16},{112,32},{1... | collective-permute-start | bytes 196616 | tf_op jit(solution)/shard_map/ppermute | solution.py:261
  20.0 6.7 %collective-permute-start.4 = (bf16[8,32,512]{2,1,0:T(8,128)(2,1)S(1)}, bf16[8,32,512]{2,1,0:T(8,128)(2,1)S(1)}, u32[]{:S(2)}, u32[]{:S(2)}) collective-permute-start(bf16[8,32,512]{2,1,0:T(8,128)(2,1)S(1)} %joined.6.refs_0_), channel_id=1, source_target_pairs={{0,128},{16,144},{32,160},{48,176},{64,192},{80,208},{96,224},{112... | collective-permute-start | bytes 786440 | tf_op jit(solution)/shard_map/ppermute | solution.py:256
  21.6 4.9 %copy-start.4 = (f32[8192]{0:T(1024)S(1)}, f32[8192]{0:T(1024)}, u32[]{:S(2)}) copy-start(f32[8192]{0:T(1024)} %param.11) | copy-start | bytes 98308
  27.6 3.3 %collective-permute-start.5 = (bf16[8,528,128]{2,1,0:T(8,128)(2,1)S(1)}, bf16[8,528,128]{2,1,0:T(8,128)(2,1)S(1)}, u32[]{:S(2)}, u32[]{:S(2)}) collective-permute-start(bf16[8,528,128]{2,1,0:T(8,128)(2,1)S(1)} %project.2), channel_id=1, source_target_pairs={{0,1},{1,0},{2,3},{3,2},{4,5},{5,4},{6,7},{7,6},{8,9},{9,8},{10,11... | collective-permute-start | bytes 3244040 | tf_op jit(solution)/shard_map/ppermute | solution.py:256
  31.1 25.0 %copy-start.2 = (bf16[128,512]{1,0:T(8,128)(2,1)S(1)}, bf16[128,512]{1,0:T(8,128)(2,1)}, u32[]{:S(2)}) copy-start(bf16[128,512]{1,0:T(8,128)(2,1)} %want.1) | copy-start | bytes 393220
  76.2 2.7 %collective-permute-start.6 = (bf16[8,528,128]{2,1,0:T(8,128)(2,1)S(1)}, bf16[8,528,128]{2,1,0:T(8,128)(2,1)S(1)}, u32[]{:S(2)}, u32[]{:S(2)}) collective-permute-start(bf16[8,528,128]{2,1,0:T(8,128)(2,1)S(1)} %all_to_all.16.refs_0_), channel_id=1, source_target_pairs={{0,1},{1,0},{2,3},{3,2},{4,5},{5,4},{6,7},{7,6},{8,9},{9,8},{10,11... | collective-permute-start | bytes 3244040 | tf_op jit(solution)/shard_map/ppermute | solution.py:256
